TPU v7x, 128 devices: a whole 4x4x4 slice. The times are simulated.
128 devices in a mesh: gz: 8 (over z, x_lo), gy: 16 (over y, x_hi, core).
Axes of the slice: x: 4 (x_hi: 2, x_lo: 2; x = x_hi * 2 + x_lo), y: 4, z: 4, core: 2. Of those that a mesh axis runs over, the one named last changes fastest.
Arguments:
- prior: float32 [8, 128, 512, 256], P(None, 'gz', 'gy'), may hold values from 0 to 1
- levels: int32 [3, 128, 512, 256], P(None, 'gz', 'gy'), may hold values from 0 to 255
- seeds: int32 [128, 512, 256], P('gz', 'gy'), may hold values from 0 to 8, as said below
- bclass: int32 [8, 16], P('gz', 'gy'), may hold values from 0 to 3
Outputs:
- probs: float32 [8, 128, 512, 256], P(None, 'gz', 'gy')
Inputs may be any that keep to these rules, and one draw needn't show every extreme that they name: `seeds`: 0 marks an unseeded voxel; k >= 1 fixes the voxel to label k - 1.
All inputs are finite; a program needn't handle non-finite values.
Results may differ from a plain program's by a relative error of at most 0.0003.
Values sent between devices are 32-bit elements; how exact they have to be, the bound alone decides.
No kernel may reach another device: no remote copies, remote signals or barrier semaphores. Data moves between devices by JAX's collectives and lax.ppermute only.
A program may use at most 64 MiB of HBM per device.

v0:
```python
import jax
import jax.numpy as jnp
from jax import lax
from jax.sharding import PartitionSpec as P

OUTER = 2


BETAS = (2.0, 4.0, 6.0, 8.0)
OMEGA = 0.8
FLOOR = 0.02


def with_halo(cells, sides, width):
    for axis, dim in sides:
        count = lax.axis_size(axis)
        ends = count - 1
        head = lax.slice_in_dim(cells, 0, width, axis=dim)
        tail = lax.slice_in_dim(cells, cells.shape[dim] - width, cells.shape[dim], axis=dim)
        cells = jnp.concatenate(
            [
                lax.ppermute(tail, axis, [(i, (i + 1) % count) for i in range(ends)]),
                cells,
                lax.ppermute(head, axis, [((i + 1) % count, i) for i in range(ends)]),
            ],
            axis=dim,
        )
    return cells


def passed_along(block, axis, distance):
    devices = range(lax.axis_size(axis))
    route = [(i - distance, i) for i in devices if i - distance in devices]
    return lax.ppermute(block, axis, route)


def start_faces(field, depth):
    ywide = with_halo(field, (("gy", 2),), depth)
    zpadded = with_halo(ywide, (("gz", 1),), 1)
    zlow = zpadded[:, :1]
    zhigh = zpadded[:, -1:]
    return (ywide, zlow, zhigh)


def per_device(prior, levels, seeds, bclass):
    brick_class = bclass[0, 0]
    beta = jnp.float32(0.0)
    for index in range(4):
        beta = beta + jnp.where(brick_class == index, BETAS[index], 0.0).astype(jnp.float32)
    ratio = levels.astype(jnp.float32) / 255.0
    weights = FLOOR + jnp.exp(-beta * ratio * ratio)
    wz, wy, wx = (weights[0], weights[1], weights[2])
    shape = wz.shape
    zidx = lax.broadcasted_iota(jnp.int32, shape, 0)
    yidx = lax.broadcasted_iota(jnp.int32, shape, 1)
    xidx = lax.broadcasted_iota(jnp.int32, shape, 2)
    top_slab = lax.axis_index("gz") == lax.axis_size("gz") - 1
    top_band = lax.axis_index("gy") == lax.axis_size("gy") - 1
    wz_up = jnp.where((zidx == shape[0] - 1) & top_slab, 0.0, wz)
    wy_up = jnp.where((yidx == shape[1] - 1) & top_band, 0.0, wy)
    wx_up = jnp.where(xidx == shape[2] - 1, 0.0, wx)
    rim_z = passed_along(wz_up[-1:], "gz", 1)
    rim_y = passed_along(wy_up[:, -1:], "gy", 1)
    wz_dn = jnp.concatenate([rim_z, wz_up[:-1]], 0)
    wy_dn = jnp.concatenate([rim_y, wy_up[:, :-1]], 1)
    wx_dn = jnp.concatenate([jnp.zeros(shape[:2] + (1,), jnp.float32), wx_up[:, :, :-1]], 2)
    degree = wz_up + wz_dn + wy_up + wy_dn + wx_up + wx_dn
    seeded = seeds > 0
    label_ids = lax.broadcasted_iota(jnp.int32, (prior.shape[0], 1, 1, 1), 0)
    onehot = (seeds[None] == label_ids + 1).astype(jnp.float32)
    zero_col = jnp.zeros(prior.shape[:3] + (1,), jnp.float32)

    def relax(field, zlow, zhigh, ypad):
        zpad = jnp.concatenate([zlow, field, zhigh], 1)
        xnext = jnp.concatenate([field[:, :, :, 1:], zero_col], 3)
        xprev = jnp.concatenate([zero_col, field[:, :, :, :-1]], 3)
        total = wz_up * zpad[:, 2:] + wz_dn * zpad[:, :-2]
        total = total + wy_up * ypad[:, :, 2:] + wy_dn * ypad[:, :, :-2]
        total = total + wx_up * xnext + wx_dn * xprev
        relaxed = (1.0 - OMEGA) * field + OMEGA * total / degree
        return jnp.where(seeded, onehot, relaxed)

    field = prior
    for outer in range(OUTER):
        ypad, zlow, zhigh = start_faces(field, 1)
        zlow = zlow[:, :, 1:-1]
        zhigh = zhigh[:, :, 1:-1]
        field = relax(field, zlow, zhigh, ypad)
        ypad = with_halo(field, (("gy", 2),), 1)
        field = relax(field, zlow, zhigh, ypad)
    return field


def solution(mesh):
    placed = (
        P(None, "gz", "gy", None),
        P(None, "gz", "gy", None),
        P("gz", "gy", None),
        P("gz", "gy"),
    )
    return jax.shard_map(
        per_device, mesh=mesh, in_specs=placed, out_specs=P(None, "gz", "gy", None), check_vma=False
    )
```

profile of v0, /device:TPU:26, one launch (start us, length us, event | category | flops | bytes accessed | tf_op | source)
XLA Modules:
  0.0 137.9 jit_solution(8315478240414621372)
XLA Ops:
  4.8 3.8 %collective-permute-start.3 = (f32[1,32,256]{2,1,0:T(8,128)S(1)}, f32[1,32,256]{2,1,0:T(8,128)S(1)}, u32[]{:S(2)}, u32[]{:S(2)}) collective-permute-start(f32[1,32,256]{2,1,0:T(8,128)S(1)} %slice.213), channel_id=1, source_target_pairs={{0,16},{16,32},{32,48},{48,64},{64,80},{80,96},{96,112},{1,17},{17... | collective-permute-start | bytes 98312 | tf_op jit(solution)/shard_map/ppermute | solution.py:34
  8.6 2.4 %copy.27 = f32[8,16,32,256]{3,1,2,0:T(8,128)S(1)} copy(f32[8,16,32,256]{3,2,1,0:T(8,128)S(1)} %copy-done) | data formatting | bytes 8388608 | tf_op args[0]
  11.0 5.2 %collective-permute-start.1 = (f32[8,16,1,256]{3,1,2,0:T(8,128)S(1)}, f32[8,16,1,256]{3,1,2,0:T(8,128)S(1)}, u32[]{:S(2)}, u32[]{:S(2)}) collective-permute-start(f32[8,16,1,256]{3,1,2,0:T(8,128)S(1)} %get-tuple-element.23), channel_id=1, source_target_pairs={{1,0},{2,1},{3,2},{4,3},{5,4},{6,5},{7,6},{8,7},{9,8},{10,9},{11,1... | collective-permute-start | bytes 393224 | tf_op jit(solution)/shard_map/ppermute | solution.py:24
  18.3 4.8 %fusion.56 = (f32[8,16,32,255]{3,1,2,0:T(8,128)}, f32[8,16,32,255]{3,1,2,0:T(8,128)}) fusion(f32[8,16,32,256]{3,1,2,0:T(8,128)S(1)} %copy.27), kind=kLoop, calls=%fused_computation.97 | loop fusion | bytes 16711680 | tf_op jit(solution)/shard_map/slice | solution.py:75
  26.0 3.5 %copy_dynamic-update-slice_fusion = f32[8,16,34,256]{3,0,2,1:T(8,128)S(1)} fusion(f32[8,16,34,256]{3,0,2,1:T(8,128)S(1)} %copy_dynamic-update-slice_fusion.2, f32[8,16,32,256]{3,2,1,0:T(8,128)S(1)} %copy-done), kind=kLoop, calls=%fused_computation.68 | loop fusion | bytes 8388608
  29.7 3.3 %collective-permute-start.2 = (f32[8,1,34,256]{3,0,2,1:T(8,128)S(1)}, f32[8,1,34,256]{3,0,2,1:T(8,128)S(1)}, u32[]{:S(2)}, u32[]{:S(2)}) collective-permute-start(f32[8,1,34,256]{3,0,2,1:T(8,128)S(1)} %get-tuple-element.9), channel_id=1, source_target_pairs={{16,0},{32,16},{48,32},{64,48},{80,64},{96,80},{112,96},{17,1},{33... | collective-permute-start | bytes 835592 | tf_op jit(solution)/shard_map/ppermute | solution.py:24
  33.0 3.7 %collective-permute-start.4 = (f32[8,1,34,256]{3,0,2,1:T(8,128)S(1)}, f32[8,1,34,256]{3,0,2,1:T(8,128)S(1)}, u32[]{:S(2)}, u32[]{:S(2)}) collective-permute-start(f32[8,1,34,256]{3,0,2,1:T(8,128)S(1)} %get-tuple-element.10), channel_id=1, source_target_pairs={{0,16},{16,32},{32,48},{48,64},{64,80},{80,96},{96,112},{1,17},{17... | collective-permute-start | bytes 835592 | tf_op jit(solution)/shard_map/ppermute | solution.py:22
  40.5 4.7 %collective-permute-done.4 = f32[8,1,34,256]{3,0,2,1:T(8,128)S(1)} collective-permute-done((f32[8,1,34,256]{3,0,2,1:T(8,128)S(1)}, f32[8,1,34,256]{3,0,2,1:T(8,128)S(1)}, u32[]{:S(2)}, u32[]{:S(2)}) %collective-permute-start.4) | collective-permute-done | bytes 278560 | tf_op jit(solution)/shard_map/ppermute | solution.py:22
  46.2 7.4 %convert_select_fusion.3 = f32[8,16,32,256]{3,1,2,0:T(8,128)S(1)} fusion(f32[8,16,32,255]{3,1,2,0:T(8,128)} %get-tuple-element.26, f32[8,16,32,255]{3,1,2,0:T(8,128)} %get-tuple-element.25, f32[8,16,32,256]{3,1,2,0:T(8,128)S(1)} %copy.27, f32[8,16,1,256]{3,1,2,0:T(8,128)} %copy-done.5, f32[8,16,1,256]{3,1,2,0:T(8,128)} %copy-done.4, ...), kind=kLoop, calls=%fused_computation.3 | loop fusion | flops 23068672 | bytes 21856288 | tf_op jit(solution)/shard_map/jit(_where)/select_n | solution.py:81
  53.6 4.0 %collective-permute-start.6 = (f32[8,16,1,256]{3,1,2,0:T(8,128)S(1)}, f32[8,16,1,256]{3,1,2,0:T(8,128)S(1)}, u32[]{:S(2)}, u32[]{:S(2)}) collective-permute-start(f32[8,16,1,256]{3,1,2,0:T(8,128)S(1)} %get-tuple-element.19), channel_id=1, source_target_pairs={{1,0},{2,1},{3,2},{4,3},{5,4},{6,5},{7,6},{8,7},{9,8},{10,9},{11,1... | collective-permute-start | bytes 393224 | tf_op jit(solution)/shard_map/ppermute | solution.py:24
  59.6 4.8 %fusion.54 = (f32[8,16,32,255]{3,1,2,0:T(8,128)}, f32[8,16,32,255]{3,1,2,0:T(8,128)}) fusion(f32[8,16,32,256]{3,1,2,0:T(8,128)S(1)} %convert_select_fusion.3), kind=kLoop, calls=%fused_computation.95 | loop fusion | bytes 16711680 | tf_op jit(solution)/shard_map/slice | solution.py:75
  64.4 2.0 %collective-permute-done.7 = f32[8,16,1,256]{3,1,2,0:T(8,128)S(1)} collective-permute-done((f32[8,16,1,256]{3,1,2,0:T(8,128)S(1)}, f32[8,16,1,256]{3,1,2,0:T(8,128)S(1)}, u32[]{:S(2)}, u32[]{:S(2)}) %collective-permute-start.7) | collective-permute-done | bytes 131104 | tf_op jit(solution)/shard_map/ppermute | solution.py:22
  67.0 7.4 %convert_select_fusion.2 = f32[8,16,32,256]{3,1,2,0:T(8,128)S(1)} fusion(f32[8,16,32,255]{3,1,2,0:T(8,128)} %get-tuple-element.22, f32[8,16,32,255]{3,1,2,0:T(8,128)} %get-tuple-element.21, f32[8,16,32,256]{3,1,2,0:T(8,128)S(1)} %convert_select_fusion.3, f32[8,16,1,256]{3,1,2,0:T(8,128)} %copy-done.9, f32[8,16,1,256]{3,1,2,0:T(8,128)} %copy-done.8, ...), kind=kLoop, calls=%fused_computation.2 | loop fusion | flops 23068672 | bytes 21856288 | tf_op jit(solution)/shard_map/jit(_where)/select_n | solution.py:81
  74.5 4.2 %collective-permute-start.9 = (f32[8,16,1,256]{3,1,2,0:T(8,128)S(1)}, f32[8,16,1,256]{3,1,2,0:T(8,128)S(1)}, u32[]{:S(2)}, u32[]{:S(2)}) collective-permute-start(f32[8,16,1,256]{3,1,2,0:T(8,128)S(1)} %get-tuple-element.15), channel_id=1, source_target_pairs={{1,0},{2,1},{3,2},{4,3},{5,4},{6,5},{7,6},{8,7},{9,8},{10,9},{11,1... | collective-permute-start | bytes 393224 | tf_op jit(solution)/shard_map/ppermute | solution.py:24
  81.1 6.2 %collective-permute-done.8 = f32[8,16,1,256]{3,1,2,0:T(8,128)S(1)} collective-permute-done((f32[8,16,1,256]{3,1,2,0:T(8,128)S(1)}, f32[8,16,1,256]{3,1,2,0:T(8,128)S(1)}, u32[]{:S(2)}, u32[]{:S(2)}) %collective-permute-start.8) | collective-permute-done | bytes 131104 | tf_op jit(solution)/shard_map/ppermute | solution.py:22
  87.8 5.6 %collective-permute-start.11 = (f32[8,1,34,256]{3,0,2,1:T(8,128)S(1)}, f32[8,1,34,256]{3,0,2,1:T(8,128)S(1)}, u32[]{:S(2)}, u32[]{:S(2)}) collective-permute-start(f32[8,1,34,256]{3,0,2,1:T(8,128)S(1)} %copy.52), channel_id=1, source_target_pairs={{0,16},{16,32},{32,48},{48,64},{64,80},{80,96},{96,112},{1,17},{17... | collective-permute-start | bytes 835592 | tf_op jit(solution)/shard_map/ppermute | solution.py:22
  95.3 4.8 %fusion.52 = (f32[8,16,32,255]{3,1,2,0:T(8,128)}, f32[8,16,32,255]{3,1,2,0:T(8,128)}) fusion(f32[8,16,32,256]{3,1,2,0:T(8,128)S(1)} %convert_select_fusion.2), kind=kLoop, calls=%fused_computation.93 | loop fusion | bytes 16711680 | tf_op jit(solution)/shard_map/slice | solution.py:75
  100.4 2.7 %collective-permute-done.10 = f32[8,1,34,256]{3,0,2,1:T(8,128)S(1)} collective-permute-done((f32[8,1,34,256]{3,0,2,1:T(8,128)S(1)}, f32[8,1,34,256]{3,0,2,1:T(8,128)S(1)}, u32[]{:S(2)}, u32[]{:S(2)}) %collective-permute-start.10) | collective-permute-done | bytes 278560 | tf_op jit(solution)/shard_map/ppermute | solution.py:24
  104.1 7.4 %convert_select_fusion.1 = f32[8,16,32,256]{3,1,2,0:T(8,128)S(1)} fusion(f32[8,16,32,255]{3,1,2,0:T(8,128)} %get-tuple-element.18, f32[8,16,32,255]{3,1,2,0:T(8,128)} %get-tuple-element.17, f32[8,16,32,256]{3,1,2,0:T(8,128)S(1)} %convert_select_fusion.2, f32[8,16,1,256]{3,1,2,0:T(8,128)} %copy-done.3, f32[8,16,1,256]{3,1,2,0:T(8,128)} %copy-done.2, ...), kind=kLoop, calls=%fused_computation.1 | loop fusion | flops 23068672 | bytes 21856288 | tf_op jit(solution)/shard_map/jit(_where)/select_n | solution.py:81
  111.6 5.1 %collective-permute-start.12 = (f32[8,16,1,256]{3,1,2,0:T(8,128)S(1)}, f32[8,16,1,256]{3,1,2,0:T(8,128)S(1)}, u32[]{:S(2)}, u32[]{:S(2)}) collective-permute-start(f32[8,16,1,256]{3,1,2,0:T(8,128)S(1)} %get-tuple-element.11), channel_id=1, source_target_pairs={{1,0},{2,1},{3,2},{4,3},{5,4},{6,5},{7,6},{8,7},{9,8},{10,9},{11,1... | collective-permute-start | bytes 393224 | tf_op jit(solution)/shard_map/ppermute | solution.py:24
  116.7 2.1 %collective-permute-start.13 = (f32[8,16,1,256]{3,1,2,0:T(8,128)S(1)}, f32[8,16,1,256]{3,1,2,0:T(8,128)S(1)}, u32[]{:S(2)}, u32[]{:S(2)}) collective-permute-start(f32[8,16,1,256]{3,1,2,0:T(8,128)S(1)} %get-tuple-element.12), channel_id=1, source_target_pairs={{0,1},{1,2},{2,3},{3,4},{4,5},{5,6},{6,7},{7,8},{8,9},{9,10},{10,1... | collective-permute-start | bytes 393224 | tf_op jit(solution)/shard_map/ppermute | solution.py:22
  118.9 4.8 %fusion.50 = (f32[8,16,32,255]{3,1,2,0:T(8,128)}, f32[8,16,32,255]{3,1,2,0:T(8,128)}) fusion(f32[8,16,32,256]{3,1,2,0:T(8,128)S(1)} %convert_select_fusion.1), kind=kLoop, calls=%fused_computation.91 | loop fusion | bytes 16711680 | tf_op jit(solution)/shard_map/slice | solution.py:75
  126.1 7.4 %convert_select_fusion = f32[8,16,32,256]{3,1,2,0:T(8,128)S(1)} fusion(f32[8,16,32,255]{3,1,2,0:T(8,128)} %get-tuple-element.14, f32[8,16,32,255]{3,1,2,0:T(8,128)} %get-tuple-element.13, f32[8,16,32,256]{3,1,2,0:T(8,128)S(1)} %convert_select_fusion.1, f32[8,16,1,256]{3,1,2,0:T(8,128)} %copy-done.7, f32[8,16,1,256]{3,1,2,0:T(8,128)} %copy-done.6, ...), kind=kLoop, calls=%fused_computation | loop fusion | flops 23068672 | bytes 21856288 | tf_op jit(solution)/shard_map/jit(_where)/select_n | solution.py:81
  133.5 4.4 %copy.54 = f32[8,16,32,256]{3,2,1,0:T(8,128)} copy(f32[8,16,32,256]{3,1,2,0:T(8,128)S(1)} %convert_select_fusion) | data formatting | bytes 8388608 | tf_op jit(solution)/shard_map/jit(_where)/select_n | solution.py:81
  (75 shorter events, 25.1 us)
Async XLA Ops:
  0.7 7.9 %copy-start = (f32[8,16,32,256]{3,2,1,0:T(8,128)S(1)}, f32[8,16,32,256]{3,2,1,0:T(8,128)}, u32[]{:S(2)}) copy-start(f32[8,16,32,256]{3,2,1,0:T(8,128)} %param.4) | copy-start | bytes 12582916
  2.8 33.8 %collective-permute-start.5 = (f32[16,1,256]{2,1,0:T(1,128)S(1)}, f32[16,1,256]{2,1,0:T(1,128)S(1)}, u32[]{:S(2)}, u32[]{:S(2)}) collective-permute-start(f32[16,1,256]{2,1,0:T(1,128)S(1)} %slice.218), channel_id=1, source_target_pairs={{0,1},{1,2},{2,3},{3,4},{4,5},{5,6},{6,7},{7,8},{8,9},{9,10},{10,1... | collective-permute-start | bytes 49160 | tf_op jit(solution)/shard_map/ppermute | solution.py:34
  4.8 31.9 %collective-permute-start.3 = (f32[1,32,256]{2,1,0:T(8,128)S(1)}, f32[1,32,256]{2,1,0:T(8,128)S(1)}, u32[]{:S(2)}, u32[]{:S(2)}) collective-permute-start(f32[1,32,256]{2,1,0:T(8,128)S(1)} %slice.213), channel_id=1, source_target_pairs={{0,16},{16,32},{32,48},{48,64},{64,80},{80,96},{96,112},{1,17},{17... | collective-permute-start | bytes 98312 | tf_op jit(solution)/shard_map/ppermute | solution.py:34
  11.0 18.5 %collective-permute-start.1 = (f32[8,16,1,256]{3,1,2,0:T(8,128)S(1)}, f32[8,16,1,256]{3,1,2,0:T(8,128)S(1)}, u32[]{:S(2)}, u32[]{:S(2)}) collective-permute-start(f32[8,16,1,256]{3,1,2,0:T(8,128)S(1)} %get-tuple-element.23), channel_id=1, source_target_pairs={{1,0},{2,1},{3,2},{4,3},{5,4},{6,5},{7,6},{8,7},{9,8},{10,9},{11,1... | collective-permute-start | bytes 393224 | tf_op jit(solution)/shard_map/ppermute | solution.py:24
  16.2 9.7 %collective-permute-start = (f32[8,16,1,256]{3,1,2,0:T(8,128)S(1)}, f32[8,16,1,256]{3,1,2,0:T(8,128)S(1)}, u32[]{:S(2)}, u32[]{:S(2)}) collective-permute-start(f32[8,16,1,256]{3,1,2,0:T(8,128)S(1)} %get-tuple-element.24), channel_id=1, source_target_pairs={{0,1},{1,2},{2,3},{3,4},{4,5},{5,6},{6,7},{7,8},{8,9},{9,10},{10,1... | collective-permute-start | bytes 393224 | tf_op jit(solution)/shard_map/ppermute | solution.py:22
  18.3 4.8 %copy-start.1 = (s32[16,32,256]{2,1,0:T(8,128)S(1)}, s32[16,32,256]{2,1,0:T(8,128)}, u32[]{:S(2)}) copy-start(s32[16,32,256]{2,1,0:T(8,128)} %param.6) | copy-start | bytes 1572868
  25.9 3.6 %copy-start.5 = (f32[8,16,1,256]{3,1,2,0:T(8,128)}, f32[8,16,1,256]{3,1,2,0:T(8,128)S(1)}, u32[]{:S(2)}) copy-start(f32[8,16,1,256]{3,1,2,0:T(8,128)S(1)} %collective-permute-done) | copy-start | bytes 393220
  29.6 10.1 %copy-start.4 = (f32[8,16,1,256]{3,1,2,0:T(8,128)}, f32[8,16,1,256]{3,1,2,0:T(8,128)S(1)}, u32[]{:S(2)}) copy-start(f32[8,16,1,256]{3,1,2,0:T(8,128)S(1)} %collective-permute-done.1) | copy-start | bytes 393220
  29.7 10.5 %collective-permute-start.2 = (f32[8,1,34,256]{3,0,2,1:T(8,128)S(1)}, f32[8,1,34,256]{3,0,2,1:T(8,128)S(1)}, u32[]{:S(2)}, u32[]{:S(2)}) collective-permute-start(f32[8,1,34,256]{3,0,2,1:T(8,128)S(1)} %get-tuple-element.9), channel_id=1, source_target_pairs={{16,0},{32,16},{48,32},{64,48},{80,64},{96,80},{112,96},{17,1},{33... | collective-permute-start | bytes 835592 | tf_op jit(solution)/shard_map/ppermute | solution.py:24
  33.0 12.2 %collective-permute-start.4 = (f32[8,1,34,256]{3,0,2,1:T(8,128)S(1)}, f32[8,1,34,256]{3,0,2,1:T(8,128)S(1)}, u32[]{:S(2)}, u32[]{:S(2)}) collective-permute-start(f32[8,1,34,256]{3,0,2,1:T(8,128)S(1)} %get-tuple-element.10), channel_id=1, source_target_pairs={{0,16},{16,32},{32,48},{48,64},{64,80},{80,96},{96,112},{1,17},{17... | collective-permute-start | bytes 835592 | tf_op jit(solution)/shard_map/ppermute | solution.py:22
  53.6 10.8 %collective-permute-start.6 = (f32[8,16,1,256]{3,1,2,0:T(8,128)S(1)}, f32[8,16,1,256]{3,1,2,0:T(8,128)S(1)}, u32[]{:S(2)}, u32[]{:S(2)}) collective-permute-start(f32[8,16,1,256]{3,1,2,0:T(8,128)S(1)} %get-tuple-element.19), channel_id=1, source_target_pairs={{1,0},{2,1},{3,2},{4,3},{5,4},{6,5},{7,6},{8,7},{9,8},{10,9},{11,1... | collective-permute-start | bytes 393224 | tf_op jit(solution)/shard_map/ppermute | solution.py:24
  57.6 8.7 %collective-permute-start.7 = (f32[8,16,1,256]{3,1,2,0:T(8,128)S(1)}, f32[8,16,1,256]{3,1,2,0:T(8,128)S(1)}, u32[]{:S(2)}, u32[]{:S(2)}) collective-permute-start(f32[8,16,1,256]{3,1,2,0:T(8,128)S(1)} %get-tuple-element.20), channel_id=1, source_target_pairs={{0,1},{1,2},{2,3},{3,4},{4,5},{5,6},{6,7},{7,8},{8,9},{9,10},{10,1... | collective-permute-start | bytes 393224 | tf_op jit(solution)/shard_map/ppermute | solution.py:22
  64.4 2.0 %copy-start.8 = (f32[8,16,1,256]{3,1,2,0:T(8,128)}, f32[8,16,1,256]{3,1,2,0:T(8,128)S(1)}, u32[]{:S(2)}) copy-start(f32[8,16,1,256]{3,1,2,0:T(8,128)S(1)} %collective-permute-done.6) | copy-start | bytes 393220
  66.3 0.7 copy-start.9
  74.5 6.7 %collective-permute-start.9 = (f32[8,16,1,256]{3,1,2,0:T(8,128)S(1)}, f32[8,16,1,256]{3,1,2,0:T(8,128)S(1)}, u32[]{:S(2)}, u32[]{:S(2)}) collective-permute-start(f32[8,16,1,256]{3,1,2,0:T(8,128)S(1)} %get-tuple-element.15), channel_id=1, source_target_pairs={{1,0},{2,1},{3,2},{4,3},{5,4},{6,5},{7,6},{8,7},{9,8},{10,9},{11,1... | collective-permute-start | bytes 393224 | tf_op jit(solution)/shard_map/ppermute | solution.py:24
  78.6 8.7 %collective-permute-start.8 = (f32[8,16,1,256]{3,1,2,0:T(8,128)S(1)}, f32[8,16,1,256]{3,1,2,0:T(8,128)S(1)}, u32[]{:S(2)}, u32[]{:S(2)}) collective-permute-start(f32[8,16,1,256]{3,1,2,0:T(8,128)S(1)} %get-tuple-element.16), channel_id=1, source_target_pairs={{0,1},{1,2},{2,3},{3,4},{4,5},{5,6},{6,7},{7,8},{8,9},{9,10},{10,1... | collective-permute-start | bytes 393224 | tf_op jit(solution)/shard_map/ppermute | solution.py:22
  81.1 19.0 %copy-start.2 = (f32[8,16,1,256]{3,1,2,0:T(8,128)}, f32[8,16,1,256]{3,1,2,0:T(8,128)S(1)}, u32[]{:S(2)}) copy-start(f32[8,16,1,256]{3,1,2,0:T(8,128)S(1)} %collective-permute-done.9) | copy-start | bytes 393220
  87.3 12.8 %copy-start.3 = (f32[8,16,1,256]{3,1,2,0:T(8,128)}, f32[8,16,1,256]{3,1,2,0:T(8,128)S(1)}, u32[]{:S(2)}) copy-start(f32[8,16,1,256]{3,1,2,0:T(8,128)S(1)} %collective-permute-done.8) | copy-start | bytes 393220
  87.8 12.4 %collective-permute-start.11 = (f32[8,1,34,256]{3,0,2,1:T(8,128)S(1)}, f32[8,1,34,256]{3,0,2,1:T(8,128)S(1)}, u32[]{:S(2)}, u32[]{:S(2)}) collective-permute-start(f32[8,1,34,256]{3,0,2,1:T(8,128)S(1)} %copy.52), channel_id=1, source_target_pairs={{0,16},{16,32},{32,48},{48,64},{64,80},{80,96},{96,112},{1,17},{17... | collective-permute-start | bytes 835592 | tf_op jit(solution)/shard_map/ppermute | solution.py:22
  93.4 9.8 %collective-permute-start.10 = (f32[8,1,34,256]{3,0,2,1:T(8,128)S(1)}, f32[8,1,34,256]{3,0,2,1:T(8,128)S(1)}, u32[]{:S(2)}, u32[]{:S(2)}) collective-permute-start(f32[8,1,34,256]{3,0,2,1:T(8,128)S(1)} %copy.50), channel_id=1, source_target_pairs={{16,0},{32,16},{48,32},{64,48},{80,64},{96,80},{112,96},{17,1},{33... | collective-permute-start | bytes 835592 | tf_op jit(solution)/shard_map/ppermute | solution.py:24
  111.6 12.1 %collective-permute-start.12 = (f32[8,16,1,256]{3,1,2,0:T(8,128)S(1)}, f32[8,16,1,256]{3,1,2,0:T(8,128)S(1)}, u32[]{:S(2)}, u32[]{:S(2)}) collective-permute-start(f32[8,16,1,256]{3,1,2,0:T(8,128)S(1)} %get-tuple-element.11), channel_id=1, source_target_pairs={{1,0},{2,1},{3,2},{4,3},{5,4},{6,5},{7,6},{8,7},{9,8},{10,9},{11,1... | collective-permute-start | bytes 393224 | tf_op jit(solution)/shard_map/ppermute | solution.py:24
  116.7 8.7 %collective-permute-start.13 = (f32[8,16,1,256]{3,1,2,0:T(8,128)S(1)}, f32[8,16,1,256]{3,1,2,0:T(8,128)S(1)}, u32[]{:S(2)}, u32[]{:S(2)}) collective-permute-start(f32[8,16,1,256]{3,1,2,0:T(8,128)S(1)} %get-tuple-element.12), channel_id=1, source_target_pairs={{0,1},{1,2},{2,3},{3,4},{4,5},{5,6},{6,7},{7,8},{8,9},{9,10},{10,1... | collective-permute-start | bytes 393224 | tf_op jit(solution)/shard_map/ppermute | solution.py:22
  123.7 1.7 %copy-start.6 = (f32[8,16,1,256]{3,1,2,0:T(8,128)}, f32[8,16,1,256]{3,1,2,0:T(8,128)S(1)}, u32[]{:S(2)}) copy-start(f32[8,16,1,256]{3,1,2,0:T(8,128)S(1)} %collective-permute-done.12) | copy-start | bytes 393220
  125.4 0.7 copy-start.7
where the time goes:
time: 139 us; the launch traced here: 138 us
  starting transfers between devices  46.5 us (33%)
  local copies, waits for them, and re-layouts  39 us (28%)
  other arithmetic  32.9 us (24%)
  waiting for transfers between devices  18.3 us (13%)
    select_n x4, other arithmetic, relax(): return jnp.where(seeded, onehot, relaxed)  29.7 us
    ppermute x6, starting transfers between devices, with_halo(): lax.ppermute(head, axis, [((i + 1) % count, i) for i in range(ends)])  23.6 us
    slice x4, local copies, waits for them, and re-layouts, relax(): xnext = jnp.concatenate([field[:, :, :, 1:], zero_col], 3)  19.2 us
    ppermute x6, starting transfers between devices, with_halo(): lax.ppermute(tail, axis, [(i, (i + 1) % count) for i in range(ends)])  17.2 us
    ppermute x6, waiting for transfers between devices, with_halo(): lax.ppermute(tail, axis, [(i, (i + 1) % count) for i in range(ends)])  14.6 us
    unnamed x27, local copies, waits for them, and re-layouts  9.24 us
    ppermute x2, starting transfers between devices, passed_along(): return lax.ppermute(block, axis, route)  5.72 us
    select_n x1, local copies, waits for them, and re-layouts, relax(): return jnp.where(seeded, onehot, relaxed)  4.39 us
  transfers between devices with their start and end apart: 14, of which 7 were waited for; matrix products, arithmetic and copies ran while one was open for 23% of the time, Pallas kernels for 0%

commit v1 on v0

v1 whole, which is shorter than its diff:
```python
import functools

import jax
import jax.numpy as jnp
from jax import lax
from jax.experimental import pallas as pl
from jax.experimental.pallas import tpu as pltpu
from jax.sharding import PartitionSpec as P

BETAS = (2.0, 4.0, 6.0, 8.0)
OMEGA = 0.8
FLOOR = 0.02

L = 8
NP = 16
NR = 32
HX = 128
PB = NP + 2
RB = 48
PS = 2 * RB
LS = PB * PS
MIB = 1 << 20

f32 = jnp.float32
VM = pl.BlockSpec(memory_space=pltpu.VMEM)
SM = pl.BlockSpec(memory_space=pltpu.SMEM)
ANY = pl.BlockSpec(memory_space=pl.ANY)


def lanes():
    return lax.broadcasted_iota(jnp.int32, (8, HX), 1)


def rolled(a, b):
    lane = lanes()
    pa, pb = pltpu.roll(a, 1, 1), pltpu.roll(b, 1, 1)
    na, nb = pltpu.roll(a, HX - 1, 1), pltpu.roll(b, HX - 1, 1)
    return (jnp.where(lane == HX - 1, nb, na), nb), (pa, jnp.where(lane == 0, pa, pb))


def flat(ref):
    n = 1
    for d in ref.shape[:-1]:
        n *= d
    return ref.reshape(n, ref.shape[-1])


def pack_rows(a, even, near, far, per):
    af = flat(a)
    for out, start in ((near, jnp.where(even, 38, 8)), (far, jnp.where(even, 8, 38))):

        def one(l, c):
            for r in range(2):
                for h in range(2):
                    for q in range(2):
                        base = l * LS + (8 * q + 1) * PS + h * RB + start + r
                        out[(l * 2 + r) * 2 + h, 8 * q : 8 * q + 8, :] = af[pl.ds(base, 8, stride=PS), :]
            return c

        lax.fori_loop(0, L, one, 0)


def unpack_rows(a, even, near, far):
    af = flat(a)
    for src, start in ((near, jnp.where(even, 40, 6)), (far, jnp.where(even, 6, 40))):

        def one(l, c):
            for r in range(2):
                for h in range(2):
                    for q in range(2):
                        base = l * LS + (8 * q + 1) * PS + h * RB + start + r
                        af[pl.ds(base, 8, stride=PS), :] = src[(l * 2 + r) * 2 + h, 8 * q : 8 * q + 8, :]
            return c

        lax.fori_loop(0, L, one, 0)


def pack_corners(a, zeven, near, far):
    af = flat(a)
    for out, p in ((near, jnp.where(zeven, NP, 1)), (far, jnp.where(zeven, 1, NP))):
        for h in range(2):
            for i, row in enumerate((7, 40)):
                out[h, 8 * i : 8 * i + 8, :] = af[pl.ds(p * PS + h * RB + row, L, stride=LS), :]


def unpack_corners(a, zeven, near, far):
    af = flat(a)
    for src, p in ((near, jnp.where(zeven, NP + 1, 0)), (far, jnp.where(zeven, 0, NP + 1))):
        for h in range(2):
            for i, row in enumerate((7, 40)):
                af[pl.ds(p * PS + h * RB + row, L, stride=LS), :] = src[h, 8 * i : 8 * i + 8, :]


def pack_planes(a, zeven, near, far):
    for out, p in ((near, jnp.where(zeven, NP, 1)), (far, jnp.where(zeven, 1, NP))):

        def one(l, c):
            for h in range(2):
                for r in range(0, NR, 8):
                    out[l, r : r + 8, h * HX : h * HX + HX] = a[l, p, h, 8 + r : 16 + r, :]
            return c

        lax.fori_loop(0, L, one, 0)


def unpack_planes(a, b, zeven, near, far):
    for src, p in ((near, jnp.where(zeven, NP + 1, 0)), (far, jnp.where(zeven, 0, NP + 1))):

        def one(l, c):
            for h in range(2):
                for r in range(0, NR, 8):
                    v = src[l, r : r + 8, h * HX : h * HX + HX]
                    a[l, p, h, 8 + r : 16 + r, :] = v
                    b[l, p, h, 8 + r : 16 + r, :] = v
            return c

        lax.fori_loop(0, L, one, 0)


def sweep_tile(src, dst, cf, sd, p, r0):
    co = [[cf[d, p, h, pl.ds(r0, 8), :] for h in range(2)] for d in range(6)]
    seed = [sd[p, h, pl.ds(r0, 8), :] for h in range(2)]
    rest = [jnp.where(s == 0, f32(1.0 - OMEGA), 0.0) for s in seed]
    for l in range(L):
        here = [src[l, p + 1, h, pl.ds(r0, 8), :] for h in range(2)]
        xn, xp = rolled(*here)
        for h in range(2):
            t = co[0][h] * src[l, p + 2, h, pl.ds(r0, 8), :] + co[1][h] * src[l, p, h, pl.ds(r0, 8), :]
            t = t + (co[2][h] * src[l, p + 1, h, pl.ds(r0 + 1, 8), :] + co[3][h] * src[l, p + 1, h, pl.ds(r0 - 1, 8), :])
            t = t + (co[4][h] * xn[h] + co[5][h] * xp[h])
            t = t + rest[h] * here[h]
            dst[l, p + 1, h, pl.ds(r0, 8), :] = jnp.where(seed[h] == l + 1, 1.0, t)


def wide_row(i):
    return jnp.where(i == 4, 33, 7 + 8 * i)


def sweep(src, dst, cf, sd, first, count, step, wide):
    tiles = 5 if wide else 4

    def body(i, c):
        p = first + (i // tiles) * step
        t = i % tiles
        sweep_tile(src, dst, cf, sd, p, wide_row(t) if wide else 8 + 8 * t)
        return c

    lax.fori_loop(0, count * tiles, body, 0)


def coefficients(w, sd, cf, first, count):
    def body(i, c):
        p, r0 = first + i // 5, wide_row(i % 5)
        seed = [sd[p, h, pl.ds(r0, 8), :] for h in range(2)]
        zu = [w[0, p + 1, h, pl.ds(r0, 8), :] for h in range(2)]
        zd = [w[0, p, h, pl.ds(r0, 8), :] for h in range(2)]
        yu = [w[1, p + 1, h, pl.ds(r0, 8), :] for h in range(2)]
        yd = [w[1, p + 1, h, pl.ds(r0 - 1, 8), :] for h in range(2)]
        xu = [w[2, p + 1, h, pl.ds(r0, 8), :] for h in range(2)]
        lane = lanes()
        pa, pb = (pltpu.roll(x, 1, 1) for x in xu)
        xd = [jnp.where(lane == 0, 0.0, pa), jnp.where(lane == 0, pa, pb)]
        for h in range(2):
            degree = zu[h] + zd[h] + yu[h] + yd[h] + xu[h] + xd[h]
            live = (seed[h] == 0) & (degree > 0.0)
            scale = jnp.where(live, OMEGA / jnp.where(live, degree, 1.0), 0.0)
            for d, x in enumerate((zu, zd, yu, yd, xu, xd)):
                cf[d, p, h, pl.ds(r0, 8), :] = scale * x[h]
        return c

    lax.fori_loop(0, count * 5, body, 0)


def k_load(at, bclass, prior, levels, seeds, a, w, sd, near, far, lev, sem):
    even, top_slab, top_band = at[0] == 0, at[2] == 1, at[3] == 1
    copies = []
    for h in range(2):
        cols = pl.ds(h * HX, HX)
        copies.append(pltpu.make_async_copy(levels.at[:, :, :, cols], lev.at[:, :, h], sem.at[2 * h]))
        copies.append(pltpu.make_async_copy(seeds.at[:, :, cols], sd.at[:, h, pl.ds(8, NR), :], sem.at[2 * h + 1]))
    for h in range(2):
        cols = pl.ds(h * HX, HX)
        for l in range(L):
            copies.append(
                pltpu.make_async_copy(
                    prior.at[l, :, :, cols], a.at[l, pl.ds(1, NP), h, pl.ds(8, NR), :], sem.at[4 + h * L + l]
                )
            )
    for c in copies:
        c.start()
    cls = bclass[0, 0]
    beta = f32(0.0)
    for index in range(4):
        beta = beta + jnp.where(cls == index, f32(BETAS[index]), f32(0.0))
    for c in copies[:4]:
        c.wait()
    row = lax.broadcasted_iota(jnp.int32, (8, HX), 0)
    lane = lanes()

    def weigh(i, c):
        p, t = i // 4, i % 4
        r0 = pl.multiple_of(8 * t, 8)
        for d in range(3):
            for h in range(2):
                ratio = lev[d, p, h, pl.ds(r0, 8), :].astype(f32) / 255.0
                x = FLOOR + jnp.exp(-beta * ratio * ratio)
                if d == 0:
                    x = jnp.where(top_slab & (p == NP - 1), 0.0, x)
                elif d == 1:
                    x = jnp.where((row == 7) & (top_band & (t == 3)), 0.0, x)
                elif h == 1:
                    x = jnp.where(lane == HX - 1, 0.0, x)
                w[d, p + 1, h, pl.ds(r0 + 8, 8), :] = x
        return c

    lax.fori_loop(0, NP * 4, weigh, 0)
    for c in copies[4:]:
        c.wait()
    pack_rows(a, even, near, far, 21)
    wf, sf = flat(w), flat(sd)
    for out, edge, other in (
        (near, jnp.where(even, 39, 8), jnp.where(even, 38, 9)),
        (far, jnp.where(even, 8, 39), jnp.where(even, 9, 38)),
    ):
        for h in range(2):
            for q in range(2):
                cut = slice(8 * q, 8 * q + 8)
                for i, (d, rw) in enumerate(((0, edge), (2, edge), (1, edge), (1, other))):
                    out[32 + 2 * i + h, cut, :] = wf[pl.ds((d * PB + 8 * q + 1) * PS + h * RB + rw, 8, stride=PS), :]
                out[40 + h, cut, :] = sf[pl.ds(8 * q * PS + h * RB + edge, 8, stride=PS), :].astype(f32)


def k_rows(at, near, far, a_in, w_in, sd_in, a, w, sd, cnear, cfar):
    even, zeven = at[0] == 0, at[1] == 0
    unpack_rows(a, even, near, far)
    wf, sf = flat(w), flat(sd)
    for src, edge, other in (
        (near, jnp.where(even, 40, 7), jnp.where(even, 41, 6)),
        (far, jnp.where(even, 7, 40), jnp.where(even, 6, 41)),
    ):
        for h in range(2):
            for q in range(2):
                cut = slice(8 * q, 8 * q + 8)
                for i, (d, rw) in enumerate(((0, edge), (2, edge), (1, edge), (1, other))):
                    wf[pl.ds((d * PB + 8 * q + 1) * PS + h * RB + rw, 8, stride=PS), :] = src[32 + 2 * i + h, cut, :]
                sf[pl.ds(8 * q * PS + h * RB + edge, 8, stride=PS), :] = src[40 + h, cut, :].astype(jnp.int32)
    pack_corners(a, zeven, cnear, cfar)
    for out in (cnear, cfar):
        for h in range(2):
            for t in range(5):
                r0 = 7 + 8 * t if t < 4 else 33
                out[h, r0 + 9 : r0 + 17, :] = w[0, NP, h, r0 : r0 + 8, :]


def k_inner(at, a_in, w, sd, a, b, cf):
    coefficients(w, sd, cf, 1, NP - 1)
    sweep(a, b, cf, sd, 1, NP - 2, 1, True)
    sweep(b, a, cf, sd, 2, NP - 4, 1, False)


def k_outer(at, znear, zfar, cnear, cfar, w_in, sd, a_in, b_in, cf_in, w, a, b, cf, near, far, pnear, pfar):
    even, zeven = at[0] == 0, at[1] == 0
    unpack_planes(a, b, zeven, znear, zfar)
    unpack_corners(a, zeven, cnear, cfar)
    for h in range(2):
        for t in range(5):
            r0 = 7 + 8 * t if t < 4 else 33
            cut = slice(r0 + 9, r0 + 17)
            w[0, 0, h, r0 : r0 + 8, :] = jnp.where(zeven, cfar[h, cut, :], cnear[h, cut, :])
    coefficients(w, sd, cf, 0, 1)
    sweep(a, b, cf, sd, 0, 2, NP - 1, True)
    sweep(b, a, cf, sd, 0, 2, 1, False)
    sweep(b, a, cf, sd, NP - 2, 2, 1, False)
    pack_planes(a, zeven, pnear, pfar)
    pack_rows(a, even, near, far, 16)


def k_rows2(at, near, far, a_in, a, cnear, cfar):
    even, zeven = at[0] == 0, at[1] == 0
    unpack_rows(a, even, near, far)
    pack_corners(a, zeven, cnear, cfar)


def put(a, out, sem, spans):
    copies = []
    for k, (first, count) in enumerate(spans):
        for h in range(2):
            for l in range(L):
                copies.append(
                    pltpu.make_async_copy(
                        a.at[l, pl.ds(1 + first, count), h, pl.ds(8, NR), :],
                        out.at[l, pl.ds(first, count), :, pl.ds(h * HX, HX)],
                        sem.at[(k * 2 + h) * L + l],
                    )
                )
    for c in copies:
        c.start()
    for c in copies:
        c.wait()


def k_inner2(at, a_in, b_in, cf, sd, a, b, out, sem):
    sweep(a, b, cf, sd, 1, NP - 2, 1, True)
    sweep(b, a, cf, sd, 2, NP - 4, 1, False)
    put(a, out, sem, ((2, NP - 4),))


def k_outer2(at, znear, zfar, cnear, cfar, cf, sd, a_in, b_in, out_in, a, b, out, sem):
    zeven = at[1] == 0
    unpack_planes(a, b, zeven, znear, zfar)
    unpack_corners(a, zeven, cnear, cfar)
    sweep(a, b, cf, sd, 0, 2, NP - 1, True)
    sweep(b, a, cf, sd, 0, 2, 1, False)
    sweep(b, a, cf, sd, NP - 2, 2, 1, False)
    put(a, out, sem, ((0, 2), (NP - 2, 2)))


def vmem(shape, dtype=f32):
    return pltpu.VMEM(shape, dtype)


A_SHAPE = (L, PB, 2, RB, HX)
W_SHAPE = (3, PB, 2, RB, HX)
S_SHAPE = (NP, 2, RB, HX)
C_SHAPE = (6, NP, 2, RB, HX)


def call(kernel, ins, outs, *, aliases=None, scratch=(), cost=3000000):
    specs = []
    for kind, _ in ins:
        specs.append({"s": SM, "v": VM, "a": ANY}[kind])
    return pl.pallas_call(
        kernel,
        out_shape=tuple(o for _, o in outs),
        in_specs=specs,
        out_specs=tuple({"v": VM, "a": ANY}[k] for k, _ in outs),
        input_output_aliases=aliases or {},
        scratch_shapes=list(scratch),
        name=kernel.__name__,
        cost_estimate=pl.CostEstimate(flops=cost, bytes_accessed=cost, transcendentals=0),
        compiler_params=pltpu.CompilerParams(vmem_limit_bytes=32 * MIB),
    )(*(x for _, x in ins))


def swaps(n):
    near = [(i, i ^ 1) for i in range(n)]
    far = []
    for i in range(1, n - 1, 2):
        far += [(i, i + 1), (i + 1, i)]
    return near, far


def per_device(prior, levels, seeds, bclass):
    iz, iy = lax.axis_index("gz"), lax.axis_index("gy")
    nz, ny = lax.axis_size("gz"), lax.axis_size("gy")
    at = jnp.stack([iy & 1, iz & 1, (iz == nz - 1).astype(jnp.int32), (iy == ny - 1).astype(jnp.int32)])
    znear_, zfar_ = swaps(nz)
    ynear_, yfar_ = swaps(ny)

    def zswap(near, far):
        far = lax.ppermute(far, "gz", zfar_)
        return lax.ppermute(near, "gz", znear_), far

    def yswap(near, far):
        far = lax.ppermute(far, "gy", yfar_)
        return lax.ppermute(near, "gy", ynear_), far

    sds = jax.ShapeDtypeStruct
    zeven = (iz & 1) == 0
    pn = lax.dynamic_index_in_dim(prior, jnp.where(zeven, NP - 1, 0), 1, keepdims=False)
    pf = lax.dynamic_index_in_dim(prior, jnp.where(zeven, 0, NP - 1), 1, keepdims=False)

    rows = sds((42, NP, HX), f32)
    a, w, sd, near, far = call(
        k_load,
        [("s", at), ("s", bclass), ("a", prior), ("a", levels), ("a", seeds)],
        [("v", vmem(A_SHAPE)), ("v", vmem(W_SHAPE)), ("v", vmem(S_SHAPE, jnp.int32)), ("v", rows), ("v", rows)],
        scratch=[pltpu.VMEM((3, NP, 2, NR, HX), jnp.int32), pltpu.SemaphoreType.DMA((20,))],
    )
    near, far = yswap(near, far)
    zn, zf = zswap(pn, pf)
    corner = sds((2, 56, HX), f32)
    a, w, sd, cn, cf_ = call(
        k_rows,
        [("s", at), ("v", near), ("v", far), ("v", a), ("v", w), ("v", sd)],
        [("v", vmem(A_SHAPE)), ("v", vmem(W_SHAPE)), ("v", vmem(S_SHAPE, jnp.int32)), ("v", corner), ("v", corner)],
        aliases={3: 0, 4: 1, 5: 2},
    )
    cn, cf_ = zswap(cn, cf_)
    a, b, cf = call(
        k_inner,
        [("s", at), ("v", a), ("v", w), ("v", sd)],
        [("v", vmem(A_SHAPE)), ("v", vmem(A_SHAPE)), ("v", vmem(C_SHAPE))],
        aliases={1: 0},
        cost=30000000,
    )
    plane = sds((L, NR, 2 * HX), f32)
    rows = sds((32, NP, HX), f32)
    w, a, b, cf, near, far, pn, pf = call(
        k_outer,
        [("s", at), ("v", zn), ("v", zf), ("v", cn), ("v", cf_), ("v", w), ("v", sd), ("v", a), ("v", b), ("v", cf)],
        [("v", vmem(W_SHAPE)), ("v", vmem(A_SHAPE)), ("v", vmem(A_SHAPE)), ("v", vmem(C_SHAPE))]
        + [("v", rows), ("v", rows), ("v", plane), ("v", plane)],
        aliases={5: 0, 7: 1, 8: 2, 9: 3},
    )
    near, far = yswap(near, far)
    zn, zf = zswap(pn, pf)
    corner = sds((2, 16, HX), f32)
    a, cn, cf_ = call(
        k_rows2,
        [("s", at), ("v", near), ("v", far), ("v", a)],
        [("v", vmem(A_SHAPE)), ("v", corner), ("v", corner)],
        aliases={3: 0},
    )
    cn, cf_ = zswap(cn, cf_)
    whole = sds(prior.shape, f32)
    a, b, out = call(
        k_inner2,
        [("s", at), ("v", a), ("v", b), ("v", cf), ("v", sd)],
        [("v", vmem(A_SHAPE)), ("v", vmem(A_SHAPE)), ("a", whole)],
        aliases={1: 0, 2: 1},
        scratch=[pltpu.SemaphoreType.DMA((16,))],
        cost=30000000,
    )
    a, b, out = call(
        k_outer2,
        [("s", at), ("v", zn), ("v", zf), ("v", cn), ("v", cf_), ("v", cf), ("v", sd), ("v", a), ("v", b), ("a", out)],
        [("v", vmem(A_SHAPE)), ("v", vmem(A_SHAPE)), ("a", whole)],
        aliases={7: 0, 8: 1, 9: 2},
        scratch=[pltpu.SemaphoreType.DMA((32,))],
    )
    return out


def solution(mesh):
    placed = (
        P(None, "gz", "gy", None),
        P(None, "gz", "gy", None),
        P("gz", "gy", None),
        P("gz", "gy"),
    )
    return jax.shard_map(
        per_device, mesh=mesh, in_specs=placed, out_specs=P(None, "gz", "gy", None), check_vma=False
    )
```

time: 139 us -> 104 us (0.75)
  Pallas kernels: 0 us -> 52.8 us
  other arithmetic: 32.9 us -> 0.08 us
  local copies, waits for them, and re-layouts: 39 us -> 12.2 us
  starting transfers between devices: 46.5 us -> 29.1 us
  waiting for transfers between devices: 18.3 us -> 8.53 us
    pallas_call x0 -> x7, Pallas kernels: none -> 52.8 us  [call(): pl.pallas_call(kernel, out_shape=tuple((o for _, o in outs)), in_specs=sp...]
    select_n x5 -> x0, other arithmetic: 29.9 us -> none  [the longest x4 29.7 us: relax(): return jnp.where(seeded, onehot, relaxed)]
    slice x20 -> x0, local copies, waits for them, and re-layouts: 20.8 us -> none  [the longest x4 19.2 us: relax(): xnext = jnp.concatenate([field[:, :, :, 1:], zero_col], 3)]
    ppermute x14 -> x12, starting transfers between devices: 46.5 us -> 29.1 us  [the longest x4 20 us: zswap(): far = lax.ppermute(far, 'gz', zfar_)]
    ppermute x14 -> x12, waiting for transfers between devices: 18.3 us -> 8.53 us  [the longest x2 8.5 us: yswap(): far = lax.ppermute(far, 'gy', yfar_)]
    select_n x1 -> x0, local copies, waits for them, and re-layouts: 4.39 us -> none  [relax(): return jnp.where(seeded, onehot, relaxed)]
    concatenate x4 -> x0, local copies, waits for them, and re-layouts: 3.33 us -> none  [the longest x1 1.12 us: per_device(): wy_dn = jnp.concatenate([rim_y, wy_up[:, :-1]], 1)]
    add x3 -> x0, other arithmetic: 2.42 us -> none  [the longest x1 1.92 us: per_device(): weights = FLOOR + jnp.exp(-beta * ratio * ratio)]
  transfers between devices with their start and end apart: 14 -> 12, of which waited for: 7 -> 2; matrix products, arithmetic and copies ran while one was open for 23% -> 1% of each run, Pallas kernels for 0% -> 37%
where the time goes in v1:
time: 104 us
  Pallas kernels  52.8 us (51%)
  starting transfers between devices  29.1 us (28%)
  local copies, waits for them, and re-layouts  12.2 us (12%)
  waiting for transfers between devices  8.53 us (8%)
    pallas_call x7, Pallas kernels, call(): pl.pallas_call(kernel, out_shape=tuple((o for _, o in outs)), in_specs=sp...  52.8 us
    ppermute x4, starting transfers between devices, zswap(): far = lax.ppermute(far, 'gz', zfar_)  20 us
    unnamed x16, local copies, waits for them, and re-layouts  11.2 us
    ppermute x2, waiting for transfers between devices, yswap(): far = lax.ppermute(far, 'gy', yfar_)  8.5 us
    ppermute x2, starting transfers between devices, yswap(): far = lax.ppermute(far, 'gy', yfar_)  8.2 us
  transfers between devices with their start and end apart: 12, of which 2 were waited for; matrix products, arithmetic and copies ran while one was open for 1% of the time, Pallas kernels for 37%

profile of v1, /device:TPU:26, one launch (start us, length us, event | category | flops | bytes accessed | tf_op | source)
XLA Modules:
  0.0 103.7 jit_solution(13532758459315865494)
XLA Ops:
  0.7 2.2 %copy-done.4 = f32[8,16,32,256]{3,2,1,0:T(8,128)S(1)} copy-done((f32[8,16,32,256]{3,2,1,0:T(8,128)S(1)}, f32[8,16,32,256]{3,2,1,0:T(8,128)}, u32[]{:S(2)}) %copy-start.4) | copy-done | bytes 4194328
  2.9 1.4 %copy-done.5 = s32[3,16,32,256]{3,2,1,0:T(8,128)S(1)} copy-done((s32[3,16,32,256]{3,2,1,0:T(8,128)S(1)}, s32[3,16,32,256]{3,2,1,0:T(8,128)}, u32[]{:S(2)}) %copy-start.5) | copy-done | bytes 1572888
  4.3 1.0 %copy-done.6 = s32[16,32,256]{2,1,0:T(8,128)S(1)} copy-done((s32[16,32,256]{2,1,0:T(8,128)S(1)}, s32[16,32,256]{2,1,0:T(8,128)}, u32[]{:S(2)}) %copy-start.6) | copy-done | bytes 524312
  5.4 4.0 %k_load.1 = (f32[8,18,2,48,128]{4,3,2,1,0:T(8,128)S(1)}, f32[3,18,2,48,128]{4,3,2,1,0:T(8,128)S(1)}, s32[16,2,48,128]{3,2,1,0:T(8,128)S(1)}, f32[42,16,128]{2,1,0:T(8,128)}, f32[42,16,128]{2,1,0:T(8,128)}) custom-call(s32[4]{0:T(128)S(1)} %pad_add_fusion.at, s32[1,1]{1,0:T(1,128)S(6)} %copy.33.bclass, f32[8,16,32,256]{3,2,1,0:T(8,128)S(1)} %copy-done.4, ...), custom_call_target="tpu_custom_call" | custom-call | flops 3000000 | bytes 3000000 | tf_op jit(solution)/shard_map/k_load/pallas_call | solution.py:332
  9.4 2.9 %copy-done = f32[8,18,2,48,128]{4,3,2,1,0:T(8,128)} copy-done((f32[8,18,2,48,128]{4,3,2,1,0:T(8,128)}, f32[8,18,2,48,128]{4,3,2,1,0:T(8,128)S(1)}, u32[]{:S(2)}) %copy-start) | copy-done | bytes 7077912
  12.2 4.3 %collective-permute-start.3 = (f32[42,16,128]{2,1,0:T(8,128)}, f32[42,16,128]{2,1,0:T(8,128)}, u32[]{:S(2)}, u32[]{:S(2)}) collective-permute-start(f32[42,16,128]{2,1,0:T(8,128)} %get-tuple-element.33), channel_id=1, source_target_pairs={{1,2},{2,1},{3,4},{4,3},{5,6},{6,5},{7,8},{8,7},{9,10},{10,9},{11,... | collective-permute-start | bytes 1032200 | tf_op jit(solution)/shard_map/ppermute | solution.py:365
  16.6 1.1 %dynamic-slice_bitcast_fusion = (f32[8,32,256]{2,1,0:T(8,128)S(1)}, f32[8,32,256]{2,1,0:T(8,128)S(1)}) fusion(f32[8,16,32,256]{3,2,1,0:T(8,128)} %prior.1, s32[]{:T(128)S(6)} %select_n.11, s32[]{:T(128)S(6)} %select_n.10), kind=kLoop, calls=%fused_computation | loop fusion | bytes 1048584 | tf_op jit(solution)/shard_map/jit(dynamic_index_in_dim)/squeeze | solution.py:371
  17.6 4.7 %collective-permute-start.1 = (f32[8,32,256]{2,1,0:T(8,128)S(1)}, f32[8,32,256]{2,1,0:T(8,128)S(1)}, u32[]{:S(2)}, u32[]{:S(2)}) collective-permute-start(f32[8,32,256]{2,1,0:T(8,128)S(1)} %get-tuple-element.59), channel_id=1, source_target_pairs={{16,32},{32,16},{48,64},{64,48},{80,96},{96,80},{17,33},{33,17},{4... | collective-permute-start | bytes 786440 | tf_op jit(solution)/shard_map/ppermute | solution.py:361
  22.4 4.7 %collective-permute-done.3.far = f32[42,16,128]{2,1,0:T(8,128)} collective-permute-done((f32[42,16,128]{2,1,0:T(8,128)}, f32[42,16,128]{2,1,0:T(8,128)}, u32[]{:S(2)}, u32[]{:S(2)}) %collective-permute-start.3) | collective-permute-done | bytes 344096 | tf_op jit(solution)/shard_map/ppermute | solution.py:365
  27.2 3.0 %copy-done.1 = f32[8,18,2,48,128]{4,3,2,1,0:T(8,128)S(1)} copy-done((f32[8,18,2,48,128]{4,3,2,1,0:T(8,128)S(1)}, f32[8,18,2,48,128]{4,3,2,1,0:T(8,128)}, u32[]{:S(2)}) %copy-start.1) | copy-done | bytes 7077912
  30.2 1.7 %k_rows.1 = (f32[8,18,2,48,128]{4,3,2,1,0:T(8,128)S(1)}, f32[3,18,2,48,128]{4,3,2,1,0:T(8,128)S(1)}, s32[16,2,48,128]{3,2,1,0:T(8,128)S(1)}, f32[2,56,128]{2,1,0:T(8,128)S(1)}, f32[2,56,128]{2,1,0:T(8,128)S(1)}) custom-call(s32[4]{0:T(128)S(1)} %pad_add_fusion.at, ...), custom_call_target="tpu_custom_call", output_to_operand_aliasing={{0}: (3, {}), {1}: (4, {}), {2}: (5, {})} | custom-call | flops 3000000 | bytes 3000000 | tf_op jit(solution)/shard_map/k_rows/pallas_call | solution.py:332
  31.9 0.6 collective-permute-start.4
  32.5 4.7 %collective-permute-start.5 = (f32[2,56,128]{2,1,0:T(8,128)S(1)}, f32[2,56,128]{2,1,0:T(8,128)S(1)}, u32[]{:S(2)}, u32[]{:S(2)}) collective-permute-start(f32[2,56,128]{2,1,0:T(8,128)S(1)} %get-tuple-element.38), channel_id=1, source_target_pairs={{16,32},{32,16},{48,64},{64,48},{80,96},{96,80},{17,33},{33,17},{4... | collective-permute-start | bytes 172040 | tf_op jit(solution)/shard_map/ppermute | solution.py:361
  37.3 20.5 %k_inner.1 = (f32[8,18,2,48,128]{4,3,2,1,0:T(8,128)S(1)}, f32[8,18,2,48,128]{4,3,2,1,0:T(8,128)S(1)}, f32[6,16,2,48,128]{4,3,2,1,0:T(8,128)S(1)}) custom-call(s32[4]{0:T(128)S(1)} %pad_add_fusion.at, f32[8,18,2,48,128]{4,3,2,1,0:T(8,128)S(1)} %get-tuple-element.41.a_in, ...), custom_call_target="tpu_custom_call", output_to_operand_aliasing={{0}: (1, {})} | custom-call | flops 30000000 | bytes 30000000 | tf_op jit(solution)/shard_map/k_inner/pallas_call | solution.py:332
  57.8 0.6 copy-done.7
  58.4 5.3 %k_outer.1 = (f32[3,18,2,48,128]{4,3,2,1,0:T(8,128)S(1)}, f32[8,18,2,48,128]{4,3,2,1,0:T(8,128)S(1)}, f32[8,18,2,48,128]{4,3,2,1,0:T(8,128)S(1)}, f32[6,16,2,48,...) custom-call(s32[4]{0:T(128)S(1)} %pad_add_fusion.at, ...), custom_call_target="tpu_custom_call", output_to_operand_aliasing={{0}: (5, {}), {1}: (7, {}), {2}: (8, {}), {3}: (9, {})} | custom-call | flops 3000000 | bytes 3000000 | tf_op jit(solution)/shard_map/k_outer/pallas_call | solution.py:332
  63.8 3.9 %collective-permute-start.9 = (f32[32,16,128]{2,1,0:T(8,128)S(1)}, f32[32,16,128]{2,1,0:T(8,128)S(1)}, u32[]{:S(2)}, u32[]{:S(2)}) collective-permute-start(f32[32,16,128]{2,1,0:T(8,128)S(1)} %get-tuple-element.48), channel_id=1, source_target_pairs={{1,2},{2,1},{3,4},{4,3},{5,6},{6,5},{7,8},{8,7},{9,10},{10,9},{11,... | collective-permute-start | bytes 786440 | tf_op jit(solution)/shard_map/ppermute | solution.py:365
  67.8 5.3 %collective-permute-start.7 = (f32[8,32,256]{2,1,0:T(8,128)S(1)}, f32[8,32,256]{2,1,0:T(8,128)S(1)}, u32[]{:S(2)}, u32[]{:S(2)}) collective-permute-start(f32[8,32,256]{2,1,0:T(8,128)S(1)} %get-tuple-element.46), channel_id=1, source_target_pairs={{16,32},{32,16},{48,64},{64,48},{80,96},{96,80},{17,33},{33,17},{4... | collective-permute-start | bytes 786440 | tf_op jit(solution)/shard_map/ppermute | solution.py:361
  73.1 3.8 %collective-permute-done.9.far = f32[32,16,128]{2,1,0:T(8,128)S(1)} collective-permute-done((f32[32,16,128]{2,1,0:T(8,128)S(1)}, f32[32,16,128]{2,1,0:T(8,128)S(1)}, u32[]{:S(2)}, u32[]{:S(2)}) %collective-permute-start.9) | collective-permute-done | bytes 262176 | tf_op jit(solution)/shard_map/ppermute | solution.py:365
  76.8 1.0 k_rows2.1
  77.8 0.1 collective-permute-start.10
  77.9 5.3 %collective-permute-start.11 = (f32[2,16,128]{2,1,0:T(8,128)S(1)}, f32[2,16,128]{2,1,0:T(8,128)S(1)}, u32[]{:S(2)}, u32[]{:S(2)}) collective-permute-start(f32[2,16,128]{2,1,0:T(8,128)S(1)} %get-tuple-element.51), channel_id=1, source_target_pairs={{16,32},{32,16},{48,64},{64,48},{80,96},{96,80},{17,33},{33,17},{4... | collective-permute-start | bytes 49160 | tf_op jit(solution)/shard_map/ppermute | solution.py:361
  83.2 15.6 %k_inner2.1 = (f32[8,18,2,48,128]{4,3,2,1,0:T(8,128)S(1)}, f32[8,18,2,48,128]{4,3,2,1,0:T(8,128)S(1)}, f32[8,16,32,256]{3,2,1,0:T(8,128)}) custom-call(s32[4]{0:T(128)S(1)} %pad_add_fusion.at, f32[8,18,2,48,128]{4,3,2,1,0:T(8,128)S(1)} %get-tuple-element.53.a_in, ...), custom_call_target="tpu_custom_call", output_to_operand_aliasing={{0}: (1, {}), {1}: (2, {})} | custom-call | flops 30000000 | bytes 30000000 | tf_op jit(solution)/shard_map/k_inner2/pallas_call | solution.py:332
  98.9 4.8 %k_outer2.1 = (f32[8,18,2,48,128]{4,3,2,1,0:T(8,128)S(1)}, f32[8,18,2,48,128]{4,3,2,1,0:T(8,128)S(1)}, f32[8,16,32,256]{3,2,1,0:T(8,128)}) custom-call(s32[4]{0:T(128)S(1)} %pad_add_fusion.at, f32[8,32,256]{2,1,0:T(8,128)S(1)} %collective-permute-done.6.znear, ...), custom_call_target="tpu_custom_call", output_to_operand_aliasing={{0}: (7, {}), {1}: (8, {}), {2}: (9, {})} | custom-call | flops 3000000 | bytes 3000000 | tf_op jit(solution)/shard_map/k_outer2/pallas_call | solution.py:332
  (25 shorter events, 0.4 us)
Async XLA Ops:
  0.7 2.2 %copy-start.4 = (f32[8,16,32,256]{3,2,1,0:T(8,128)S(1)}, f32[8,16,32,256]{3,2,1,0:T(8,128)}, u32[]{:S(2)}) copy-start(f32[8,16,32,256]{3,2,1,0:T(8,128)} %prior.1) | copy-start | bytes 12582916
  2.9 1.4 %copy-start.5 = (s32[3,16,32,256]{3,2,1,0:T(8,128)S(1)}, s32[3,16,32,256]{3,2,1,0:T(8,128)}, u32[]{:S(2)}) copy-start(s32[3,16,32,256]{3,2,1,0:T(8,128)} %levels.1) | copy-start | bytes 4718596
  4.3 1.0 %copy-start.6 = (s32[16,32,256]{2,1,0:T(8,128)S(1)}, s32[16,32,256]{2,1,0:T(8,128)}, u32[]{:S(2)}) copy-start(s32[16,32,256]{2,1,0:T(8,128)} %seeds.1) | copy-start | bytes 1572868
  9.3 2.9 %copy-start = (f32[8,18,2,48,128]{4,3,2,1,0:T(8,128)}, f32[8,18,2,48,128]{4,3,2,1,0:T(8,128)S(1)}, u32[]{:S(2)}) copy-start(f32[8,18,2,48,128]{4,3,2,1,0:T(8,128)S(1)} %get-tuple-element.34.a_in) | copy-start | bytes 21233668
  12.2 10.2 %collective-permute-start.2 = (f32[42,16,128]{2,1,0:T(8,128)}, f32[42,16,128]{2,1,0:T(8,128)}, u32[]{:S(2)}, u32[]{:S(2)}) collective-permute-start(f32[42,16,128]{2,1,0:T(8,128)} %get-tuple-element.32), channel_id=1, source_target_pairs={{0,1},{1,0},{2,3},{3,2},{4,5},{5,4},{6,7},{7,6},{8,9},{9,8},{10,11... | collective-permute-start | bytes 1032200 | tf_op jit(solution)/shard_map/ppermute | solution.py:366
  12.2 15.0 %collective-permute-start.3 = (f32[42,16,128]{2,1,0:T(8,128)}, f32[42,16,128]{2,1,0:T(8,128)}, u32[]{:S(2)}, u32[]{:S(2)}) collective-permute-start(f32[42,16,128]{2,1,0:T(8,128)} %get-tuple-element.33), channel_id=1, source_target_pairs={{1,2},{2,1},{3,4},{4,3},{5,6},{6,5},{7,8},{8,7},{9,10},{10,9},{11,... | collective-permute-start | bytes 1032200 | tf_op jit(solution)/shard_map/ppermute | solution.py:365
  17.6 40.1 %collective-permute-start.1 = (f32[8,32,256]{2,1,0:T(8,128)S(1)}, f32[8,32,256]{2,1,0:T(8,128)S(1)}, u32[]{:S(2)}, u32[]{:S(2)}) collective-permute-start(f32[8,32,256]{2,1,0:T(8,128)S(1)} %get-tuple-element.59), channel_id=1, source_target_pairs={{16,32},{32,16},{48,64},{64,48},{80,96},{96,80},{17,33},{33,17},{4... | collective-permute-start | bytes 786440 | tf_op jit(solution)/shard_map/ppermute | solution.py:361
  22.3 35.4 %collective-permute-start = (f32[8,32,256]{2,1,0:T(8,128)S(1)}, f32[8,32,256]{2,1,0:T(8,128)S(1)}, u32[]{:S(2)}, u32[]{:S(2)}) collective-permute-start(f32[8,32,256]{2,1,0:T(8,128)S(1)} %get-tuple-element.60), channel_id=1, source_target_pairs={{0,16},{16,0},{32,48},{48,32},{64,80},{80,64},{96,112},{112,96},{1... | collective-permute-start | bytes 786440 | tf_op jit(solution)/shard_map/ppermute | solution.py:362
  27.2 3.0 %copy-start.1 = (f32[8,18,2,48,128]{4,3,2,1,0:T(8,128)S(1)}, f32[8,18,2,48,128]{4,3,2,1,0:T(8,128)}, u32[]{:S(2)}) copy-start(f32[8,18,2,48,128]{4,3,2,1,0:T(8,128)} %copy-done) | copy-start | bytes 21233668
  31.9 25.9 %copy-start.2 = (s32[16,2,48,128]{3,2,1,0:T(8,128)}, s32[16,2,48,128]{3,2,1,0:T(8,128)S(1)}, u32[]{:S(2)}) copy-start(s32[16,2,48,128]{3,2,1,0:T(8,128)S(1)} %get-tuple-element.40.sd) | copy-start | bytes 2359300
  31.9 25.9 %collective-permute-start.4 = (f32[2,56,128]{2,1,0:T(8,128)S(1)}, f32[2,56,128]{2,1,0:T(8,128)S(1)}, u32[]{:S(2)}, u32[]{:S(2)}) collective-permute-start(f32[2,56,128]{2,1,0:T(8,128)S(1)} %get-tuple-element.37), channel_id=1, source_target_pairs={{0,16},{16,0},{32,48},{48,32},{64,80},{80,64},{96,112},{112,96},{1... | collective-permute-start | bytes 172040 | tf_op jit(solution)/shard_map/ppermute | solution.py:362
  32.5 25.3 %collective-permute-start.5 = (f32[2,56,128]{2,1,0:T(8,128)S(1)}, f32[2,56,128]{2,1,0:T(8,128)S(1)}, u32[]{:S(2)}, u32[]{:S(2)}) collective-permute-start(f32[2,56,128]{2,1,0:T(8,128)S(1)} %get-tuple-element.38), channel_id=1, source_target_pairs={{16,32},{32,16},{48,64},{64,48},{80,96},{96,80},{17,33},{33,17},{4... | collective-permute-start | bytes 172040 | tf_op jit(solution)/shard_map/ppermute | solution.py:361
  57.7 0.7 copy-start.7
  63.7 19.5 %copy-start.3 = (s32[16,2,48,128]{3,2,1,0:T(8,128)S(1)}, s32[16,2,48,128]{3,2,1,0:T(8,128)}, u32[]{:S(2)}) copy-start(s32[16,2,48,128]{3,2,1,0:T(8,128)} %copy-done.2) | copy-start | bytes 2359300
  63.7 9.4 %collective-permute-start.8 = (f32[32,16,128]{2,1,0:T(8,128)S(1)}, f32[32,16,128]{2,1,0:T(8,128)S(1)}, u32[]{:S(2)}, u32[]{:S(2)}) collective-permute-start(f32[32,16,128]{2,1,0:T(8,128)S(1)} %get-tuple-element.47), channel_id=1, source_target_pairs={{0,1},{1,0},{2,3},{3,2},{4,5},{5,4},{6,7},{7,6},{8,9},{9,8},{10,11... | collective-permute-start | bytes 786440 | tf_op jit(solution)/shard_map/ppermute | solution.py:366
  63.8 13.0 %collective-permute-start.9 = (f32[32,16,128]{2,1,0:T(8,128)S(1)}, f32[32,16,128]{2,1,0:T(8,128)S(1)}, u32[]{:S(2)}, u32[]{:S(2)}) collective-permute-start(f32[32,16,128]{2,1,0:T(8,128)S(1)} %get-tuple-element.48), channel_id=1, source_target_pairs={{1,2},{2,1},{3,4},{4,3},{5,6},{6,5},{7,8},{8,7},{9,10},{10,9},{11,... | collective-permute-start | bytes 786440 | tf_op jit(solution)/shard_map/ppermute | solution.py:365
  67.7 31.1 %collective-permute-start.6 = (f32[8,32,256]{2,1,0:T(8,128)S(1)}, f32[8,32,256]{2,1,0:T(8,128)S(1)}, u32[]{:S(2)}, u32[]{:S(2)}) collective-permute-start(f32[8,32,256]{2,1,0:T(8,128)S(1)} %get-tuple-element.45), channel_id=1, source_target_pairs={{0,16},{16,0},{32,48},{48,32},{64,80},{80,64},{96,112},{112,96},{1... | collective-permute-start | bytes 786440 | tf_op jit(solution)/shard_map/ppermute | solution.py:362
  67.8 31.1 %collective-permute-start.7 = (f32[8,32,256]{2,1,0:T(8,128)S(1)}, f32[8,32,256]{2,1,0:T(8,128)S(1)}, u32[]{:S(2)}, u32[]{:S(2)}) collective-permute-start(f32[8,32,256]{2,1,0:T(8,128)S(1)} %get-tuple-element.46), channel_id=1, source_target_pairs={{16,32},{32,16},{48,64},{64,48},{80,96},{96,80},{17,33},{33,17},{4... | collective-permute-start | bytes 786440 | tf_op jit(solution)/shard_map/ppermute | solution.py:361
  77.8 21.0 %collective-permute-start.10 = (f32[2,16,128]{2,1,0:T(8,128)S(1)}, f32[2,16,128]{2,1,0:T(8,128)S(1)}, u32[]{:S(2)}, u32[]{:S(2)}) collective-permute-start(f32[2,16,128]{2,1,0:T(8,128)S(1)} %get-tuple-element.50), channel_id=1, source_target_pairs={{0,16},{16,0},{32,48},{48,32},{64,80},{80,64},{96,112},{112,96},{1... | collective-permute-start | bytes 49160 | tf_op jit(solution)/shard_map/ppermute | solution.py:362
  77.9 21.0 %collective-permute-start.11 = (f32[2,16,128]{2,1,0:T(8,128)S(1)}, f32[2,16,128]{2,1,0:T(8,128)S(1)}, u32[]{:S(2)}, u32[]{:S(2)}) collective-permute-start(f32[2,16,128]{2,1,0:T(8,128)S(1)} %get-tuple-element.51), channel_id=1, source_target_pairs={{16,32},{32,16},{48,64},{64,48},{80,96},{96,80},{17,33},{33,17},{4... | collective-permute-start | bytes 49160 | tf_op jit(solution)/shard_map/ppermute | solution.py:361

commit v2 on v1

--- a/solution.py
+++ b/solution.py
@@ -24,7 +24,7 @@
 f32 = jnp.float32
 VM = pl.BlockSpec(memory_space=pltpu.VMEM)
 SM = pl.BlockSpec(memory_space=pltpu.SMEM)
-ANY = pl.BlockSpec(memory_space=pl.ANY)
+ANY = pl.BlockSpec(memory_space=pltpu.HBM)
 
 
 def lanes():
@@ -117,35 +117,35 @@
         lax.fori_loop(0, L, one, 0)
 
 
-def sweep_tile(src, dst, cf, sd, p, r0):
-    co = [[cf[d, p, h, pl.ds(r0, 8), :] for h in range(2)] for d in range(6)]
-    seed = [sd[p, h, pl.ds(r0, 8), :] for h in range(2)]
-    rest = [jnp.where(s == 0, f32(1.0 - OMEGA), 0.0) for s in seed]
-    for l in range(L):
-        here = [src[l, p + 1, h, pl.ds(r0, 8), :] for h in range(2)]
-        xn, xp = rolled(*here)
-        for h in range(2):
-            t = co[0][h] * src[l, p + 2, h, pl.ds(r0, 8), :] + co[1][h] * src[l, p, h, pl.ds(r0, 8), :]
-            t = t + (co[2][h] * src[l, p + 1, h, pl.ds(r0 + 1, 8), :] + co[3][h] * src[l, p + 1, h, pl.ds(r0 - 1, 8), :])
-            t = t + (co[4][h] * xn[h] + co[5][h] * xp[h])
-            t = t + rest[h] * here[h]
-            dst[l, p + 1, h, pl.ds(r0, 8), :] = jnp.where(seed[h] == l + 1, 1.0, t)
+def sweep(src, dst, cf, sd, first, count, step, wide, onehot):
+    sf, df, kf, ef = flat(src), flat(dst), flat(cf), flat(sd)
+    starts = (7, 15, 23, 31, 33) if wide else (8, 16, 24, 32)
+
+    def body(i, c):
+        p = first + i * step
+        at, to = p * PS, (p + 1) * PS
+        for r0 in starts:
+            co = [[kf[pl.ds(at + (d * NP * 2 + h) * RB + r0, 8), :] for h in range(2)] for d in range(6)]
+            seed = [ef[pl.ds(at + h * RB + r0, 8), :] for h in range(2)]
+            rest = [jnp.where(s == 0, f32(1.0 - OMEGA), f32(0.0 if onehot else 1.0)) for s in seed]
+            for l in range(L):
+                base = to + l * LS + r0
+                here = [sf[pl.ds(base + h * RB, 8), :] for h in range(2)]
+                xn, xp = rolled(*here)
+                for h in range(2):
+                    o = base + h * RB
+                    t = co[0][h] * sf[pl.ds(o + PS, 8), :] + co[1][h] * sf[pl.ds(o - PS, 8), :]
+                    t = t + (co[2][h] * sf[pl.ds(o + 1, 8), :] + co[3][h] * sf[pl.ds(o - 1, 8), :])
+                    t = t + (co[4][h] * xn[h] + co[5][h] * xp[h])
+                    t = t + rest[h] * here[h]
+                    df[pl.ds(o, 8), :] = jnp.where(seed[h] == l + 1, 1.0, t) if onehot else t
+        return c
+
+    lax.fori_loop(0, count, body, 0)
 
 
 def wide_row(i):
     return jnp.where(i == 4, 33, 7 + 8 * i)
-
-
-def sweep(src, dst, cf, sd, first, count, step, wide):
-    tiles = 5 if wide else 4
-
-    def body(i, c):
-        p = first + (i // tiles) * step
-        t = i % tiles
-        sweep_tile(src, dst, cf, sd, p, wide_row(t) if wide else 8 + 8 * t)
-        return c
-
-    lax.fori_loop(0, count * tiles, body, 0)
 
 
 def coefficients(w, sd, cf, first, count):
@@ -171,8 +171,8 @@
     lax.fori_loop(0, count * 5, body, 0)
 
 
-def k_load(at, bclass, prior, levels, seeds, a, w, sd, near, far, lev, sem):
-    even, top_slab, top_band = at[0] == 0, at[2] == 1, at[3] == 1
+def k_load(at, bclass, prior, levels, seeds, a, w, sd, near, far, pn, pf, lev, sem):
+    even, zeven, top_slab, top_band = at[0] == 0, at[1] == 0, at[2] == 1, at[3] == 1
     copies = []
     for h in range(2):
         cols = pl.ds(h * HX, HX)
@@ -186,6 +186,8 @@
                     prior.at[l, :, :, cols], a.at[l, pl.ds(1, NP), h, pl.ds(8, NR), :], sem.at[4 + h * L + l]
                 )
             )
+    copies.append(pltpu.make_async_copy(prior.at[:, jnp.where(zeven, NP - 1, 0)], pn, sem.at[20]))
+    copies.append(pltpu.make_async_copy(prior.at[:, jnp.where(zeven, 0, NP - 1)], pf, sem.at[21]))
     for c in copies:
         c.start()
     cls = bclass[0, 0]
@@ -254,8 +256,8 @@
 
 def k_inner(at, a_in, w, sd, a, b, cf):
     coefficients(w, sd, cf, 1, NP - 1)
-    sweep(a, b, cf, sd, 1, NP - 2, 1, True)
-    sweep(b, a, cf, sd, 2, NP - 4, 1, False)
+    sweep(a, b, cf, sd, 1, NP - 2, 1, True, True)
+    sweep(b, a, cf, sd, 2, NP - 4, 1, False, False)
 
 
 def k_outer(at, znear, zfar, cnear, cfar, w_in, sd, a_in, b_in, cf_in, w, a, b, cf, near, far, pnear, pfar):
@@ -268,9 +270,9 @@
             cut = slice(r0 + 9, r0 + 17)
             w[0, 0, h, r0 : r0 + 8, :] = jnp.where(zeven, cfar[h, cut, :], cnear[h, cut, :])
     coefficients(w, sd, cf, 0, 1)
-    sweep(a, b, cf, sd, 0, 2, NP - 1, True)
-    sweep(b, a, cf, sd, 0, 2, 1, False)
-    sweep(b, a, cf, sd, NP - 2, 2, 1, False)
+    sweep(a, b, cf, sd, 0, 2, NP - 1, True, True)
+    sweep(b, a, cf, sd, 0, 2, 1, False, False)
+    sweep(b, a, cf, sd, NP - 2, 2, 1, False, False)
     pack_planes(a, zeven, pnear, pfar)
     pack_rows(a, even, near, far, 16)
 
@@ -300,8 +302,8 @@
 
 
 def k_inner2(at, a_in, b_in, cf, sd, a, b, out, sem):
-    sweep(a, b, cf, sd, 1, NP - 2, 1, True)
-    sweep(b, a, cf, sd, 2, NP - 4, 1, False)
+    sweep(a, b, cf, sd, 1, NP - 2, 1, True, False)
+    sweep(b, a, cf, sd, 2, NP - 4, 1, False, False)
     put(a, out, sem, ((2, NP - 4),))
 
 
@@ -309,9 +311,9 @@
     zeven = at[1] == 0
     unpack_planes(a, b, zeven, znear, zfar)
     unpack_corners(a, zeven, cnear, cfar)
-    sweep(a, b, cf, sd, 0, 2, NP - 1, True)
-    sweep(b, a, cf, sd, 0, 2, 1, False)
-    sweep(b, a, cf, sd, NP - 2, 2, 1, False)
+    sweep(a, b, cf, sd, 0, 2, NP - 1, True, False)
+    sweep(b, a, cf, sd, 0, 2, 1, False, False)
+    sweep(b, a, cf, sd, NP - 2, 2, 1, False, False)
     put(a, out, sem, ((0, 2), (NP - 2, 2)))
 
 
@@ -325,7 +327,7 @@
 C_SHAPE = (6, NP, 2, RB, HX)
 
 
-def call(kernel, ins, outs, *, aliases=None, scratch=(), cost=3000000):
+def call(kernel, ins, outs, *, aliases=None, scratch=(), cost=3000000, grant=4):
     specs = []
     for kind, _ in ins:
         specs.append({"s": SM, "v": VM, "a": ANY}[kind])
@@ -338,7 +340,7 @@
         scratch_shapes=list(scratch),
         name=kernel.__name__,
         cost_estimate=pl.CostEstimate(flops=cost, bytes_accessed=cost, transcendentals=0),
-        compiler_params=pltpu.CompilerParams(vmem_limit_bytes=32 * MIB),
+        compiler_params=pltpu.CompilerParams(vmem_limit_bytes=grant * MIB),
     )(*(x for _, x in ins))
 
 
@@ -365,17 +367,16 @@
         far = lax.ppermute(far, "gy", yfar_)
         return lax.ppermute(near, "gy", ynear_), far
 
+    prior, levels, seeds = (pltpu.with_memory_space_constraint(x, pltpu.HBM) for x in (prior, levels, seeds))
     sds = jax.ShapeDtypeStruct
-    zeven = (iz & 1) == 0
-    pn = lax.dynamic_index_in_dim(prior, jnp.where(zeven, NP - 1, 0), 1, keepdims=False)
-    pf = lax.dynamic_index_in_dim(prior, jnp.where(zeven, 0, NP - 1), 1, keepdims=False)
-
     rows = sds((42, NP, HX), f32)
-    a, w, sd, near, far = call(
+    plane = sds((L, NR, 2 * HX), f32)
+    a, w, sd, near, far, pn, pf = call(
         k_load,
         [("s", at), ("s", bclass), ("a", prior), ("a", levels), ("a", seeds)],
-        [("v", vmem(A_SHAPE)), ("v", vmem(W_SHAPE)), ("v", vmem(S_SHAPE, jnp.int32)), ("v", rows), ("v", rows)],
-        scratch=[pltpu.VMEM((3, NP, 2, NR, HX), jnp.int32), pltpu.SemaphoreType.DMA((20,))],
+        [("v", vmem(A_SHAPE)), ("v", vmem(W_SHAPE)), ("v", vmem(S_SHAPE, jnp.int32)), ("v", rows), ("v", rows), ("v", plane), ("v", plane)],
+        scratch=[pltpu.VMEM((3, NP, 2, NR, HX), jnp.int32), pltpu.SemaphoreType.DMA((22,))],
+        grant=8,
     )
     near, far = yswap(near, far)
     zn, zf = zswap(pn, pf)
@@ -394,7 +395,6 @@
         aliases={1: 0},
         cost=30000000,
     )
-    plane = sds((L, NR, 2 * HX), f32)
     rows = sds((32, NP, HX), f32)
     w, a, b, cf, near, far, pn, pf = call(
         k_outer,

time: 104 us -> 73.5 us (0.71)
  Pallas kernels: 52.8 us -> 33.9 us
  local copies, waits for them, and re-layouts: 12.2 us -> 0 us
    pallas_call x7, Pallas kernels: 52.8 us -> 33.9 us  [call(): pl.pallas_call(kernel, out_shape=tuple((o for _, o in outs)), in_specs=sp...]
    unnamed x16 -> x0, local copies, waits for them, and re-layouts: 11.2 us -> none
    ppermute x4, starting transfers between devices: 0.87 us -> 2.3 us  [zswap(): return (lax.ppermute(near, 'gz', znear_), far)]
    squeeze x1 -> x0, local copies, waits for them, and re-layouts: 1.08 us -> none  [per_device(): lax.dynamic_index_in_dim(prior, jnp.where(zeven, 0, NP - 1), 1, keepdims=...]
  transfers between devices with their start and end apart: 12 -> 12, of which waited for: 2 -> 2; matrix products, arithmetic and copies ran while one was open for 1% -> 0% of each run, Pallas kernels for 37% -> 32%
where the time goes in v2:
time: 73.5 us; the launch traced here: 73.2 us
  Pallas kernels  33.9 us (46%)
  starting transfers between devices  29.6 us (40%)
  waiting for transfers between devices  8.78 us (12%)
  between operations  0.86 us (1%)
    pallas_call x7, Pallas kernels, call(): pl.pallas_call(kernel, out_shape=tuple((o for _, o in outs)), in_specs=sp...  33.9 us
    ppermute x4, starting transfers between devices, zswap(): far = lax.ppermute(far, 'gz', zfar_)  19.1 us
    ppermute x2, waiting for transfers between devices, yswap(): far = lax.ppermute(far, 'gy', yfar_)  8.75 us
    ppermute x2, starting transfers between devices, yswap(): far = lax.ppermute(far, 'gy', yfar_)  8.04 us
    ppermute x4, starting transfers between devices, zswap(): return (lax.ppermute(near, 'gz', znear_), far)  2.3 us
  transfers between devices with their start and end apart: 12, of which 2 were waited for; matrix products, arithmetic and copies ran while one was open for 0% of the time, Pallas kernels for 32%

profile of v2, /device:TPU:26, one launch (start us, length us, event | category | flops | bytes accessed | tf_op | source)
XLA Modules:
  0.0 73.2 jit_solution(654947778797931358)
XLA Ops:
  0.7 0.1 pad_add_fusion.at
  0.7 4.3 %k_load.1 = (f32[8,18,2,48,128]{4,3,2,1,0:T(8,128)S(1)}, f32[3,18,2,48,128]{4,3,2,1,0:T(8,128)S(1)}, s32[16,2,48,128]{3,2,1,0:T(8,128)S(1)}, f32[42,16,128]{2,1,...) custom-call(s32[4]{0:T(128)S(1)} %pad_add_fusion.at, ...), custom_call_target="tpu_custom_call" | custom-call | flops 3000000 | bytes 3000000 | tf_op jit(solution)/shard_map/k_load/pallas_call | solution.py:334
  5.0 0.1 collective-permute-start.2
  5.1 4.3 %collective-permute-start.3 = (f32[42,16,128]{2,1,0:T(8,128)S(1)}, f32[42,16,128]{2,1,0:T(8,128)S(1)}, u32[]{:S(2)}, u32[]{:S(2)}) collective-permute-start(f32[42,16,128]{2,1,0:T(8,128)S(1)} %get-tuple-element.37), channel_id=1, source_target_pairs={{1,2},{2,1},{3,4},{4,3},{5,6},{6,5},{7,8},{8,7},{9,10},{10,9},{11,... | collective-permute-start | bytes 1032200 | tf_op jit(solution)/shard_map/ppermute | solution.py:367
  9.4 1.5 %collective-permute-start = (f32[8,32,256]{2,1,0:T(8,128)S(1)}, f32[8,32,256]{2,1,0:T(8,128)S(1)}, u32[]{:S(2)}, u32[]{:S(2)}) collective-permute-start(f32[8,32,256]{2,1,0:T(8,128)S(1)} %get-tuple-element.34), channel_id=1, source_target_pairs={{0,16},{16,0},{32,48},{48,32},{64,80},{80,64},{96,112},{112,96},{1... | collective-permute-start | bytes 786440 | tf_op jit(solution)/shard_map/ppermute | solution.py:364
  10.9 3.8 %collective-permute-start.1 = (f32[8,32,256]{2,1,0:T(8,128)S(1)}, f32[8,32,256]{2,1,0:T(8,128)S(1)}, u32[]{:S(2)}, u32[]{:S(2)}) collective-permute-start(f32[8,32,256]{2,1,0:T(8,128)S(1)} %get-tuple-element.35), channel_id=1, source_target_pairs={{16,32},{32,16},{48,64},{64,48},{80,96},{96,80},{17,33},{33,17},{4... | collective-permute-start | bytes 786440 | tf_op jit(solution)/shard_map/ppermute | solution.py:363
  14.8 0.0 collective-permute-done.2.near
  14.8 5.0 %collective-permute-done.3.far = f32[42,16,128]{2,1,0:T(8,128)S(1)} collective-permute-done((f32[42,16,128]{2,1,0:T(8,128)S(1)}, f32[42,16,128]{2,1,0:T(8,128)S(1)}, u32[]{:S(2)}, u32[]{:S(2)}) %collective-permute-start.3) | collective-permute-done | bytes 344096 | tf_op jit(solution)/shard_map/ppermute | solution.py:367
  19.8 1.1 %k_rows.1 = (f32[8,18,2,48,128]{4,3,2,1,0:T(8,128)S(1)}, f32[3,18,2,48,128]{4,3,2,1,0:T(8,128)S(1)}, s32[16,2,48,128]{3,2,1,0:T(8,128)S(1)}, f32[2,56,128]{2,1,0:T(8,128)S(1)}, f32[2,56,128]{2,1,0:T(8,128)S(1)}) custom-call(s32[4]{0:T(128)S(1)} %pad_add_fusion.at, ...), custom_call_target="tpu_custom_call", output_to_operand_aliasing={{0}: (3, {}), {1}: (4, {}), {2}: (5, {})} | custom-call | flops 3000000 | bytes 3000000 | tf_op jit(solution)/shard_map/k_rows/pallas_call | solution.py:334
  20.9 0.6 collective-permute-start.4
  21.5 4.7 %collective-permute-start.5 = (f32[2,56,128]{2,1,0:T(8,128)S(1)}, f32[2,56,128]{2,1,0:T(8,128)S(1)}, u32[]{:S(2)}, u32[]{:S(2)}) collective-permute-start(f32[2,56,128]{2,1,0:T(8,128)S(1)} %get-tuple-element.42), channel_id=1, source_target_pairs={{16,32},{32,16},{48,64},{64,48},{80,96},{96,80},{17,33},{33,17},{4... | collective-permute-start | bytes 172040 | tf_op jit(solution)/shard_map/ppermute | solution.py:363
  26.3 13.1 %k_inner.1 = (f32[8,18,2,48,128]{4,3,2,1,0:T(8,128)S(1)}, f32[8,18,2,48,128]{4,3,2,1,0:T(8,128)S(1)}, f32[6,16,2,48,128]{4,3,2,1,0:T(8,128)S(1)}) custom-call(s32[4]{0:T(128)S(1)} %pad_add_fusion.at, f32[8,18,2,48,128]{4,3,2,1,0:T(8,128)S(1)} %get-tuple-element.45.a_in, ...), custom_call_target="tpu_custom_call", output_to_operand_aliasing={{0}: (1, {})} | custom-call | flops 30000000 | bytes 30000000 | tf_op jit(solution)/shard_map/k_inner/pallas_call | solution.py:334
  39.4 0.0 collective-permute-done.1.zfar
  39.4 3.0 %k_outer.1 = (f32[3,18,2,48,128]{4,3,2,1,0:T(8,128)S(1)}, f32[8,18,2,48,128]{4,3,2,1,0:T(8,128)S(1)}, f32[8,18,2,48,128]{4,3,2,1,0:T(8,128)S(1)}, f32[6,16,2,48,...) custom-call(s32[4]{0:T(128)S(1)} %pad_add_fusion.at, ...), custom_call_target="tpu_custom_call", output_to_operand_aliasing={{0}: (5, {}), {1}: (7, {}), {2}: (8, {}), {3}: (9, {})} | custom-call | flops 3000000 | bytes 3000000 | tf_op jit(solution)/shard_map/k_outer/pallas_call | solution.py:334
  42.4 0.1 collective-permute-start.8
  42.5 3.7 %collective-permute-start.9 = (f32[32,16,128]{2,1,0:T(8,128)S(1)}, f32[32,16,128]{2,1,0:T(8,128)S(1)}, u32[]{:S(2)}, u32[]{:S(2)}) collective-permute-start(f32[32,16,128]{2,1,0:T(8,128)S(1)} %get-tuple-element.52), channel_id=1, source_target_pairs={{1,2},{2,1},{3,4},{4,3},{5,6},{6,5},{7,8},{8,7},{9,10},{10,9},{11,... | collective-permute-start | bytes 786440 | tf_op jit(solution)/shard_map/ppermute | solution.py:367
  46.2 0.1 collective-permute-start.6
  46.3 5.3 %collective-permute-start.7 = (f32[8,32,256]{2,1,0:T(8,128)S(1)}, f32[8,32,256]{2,1,0:T(8,128)S(1)}, u32[]{:S(2)}, u32[]{:S(2)}) collective-permute-start(f32[8,32,256]{2,1,0:T(8,128)S(1)} %get-tuple-element.50), channel_id=1, source_target_pairs={{16,32},{32,16},{48,64},{64,48},{80,96},{96,80},{17,33},{33,17},{4... | collective-permute-start | bytes 786440 | tf_op jit(solution)/shard_map/ppermute | solution.py:363
  51.6 3.8 %collective-permute-done.9.far = f32[32,16,128]{2,1,0:T(8,128)S(1)} collective-permute-done((f32[32,16,128]{2,1,0:T(8,128)S(1)}, f32[32,16,128]{2,1,0:T(8,128)S(1)}, u32[]{:S(2)}, u32[]{:S(2)}) %collective-permute-start.9) | collective-permute-done | bytes 262176 | tf_op jit(solution)/shard_map/ppermute | solution.py:367
  55.4 1.0 %k_rows2.1 = (f32[8,18,2,48,128]{4,3,2,1,0:T(8,128)S(1)}, f32[2,16,128]{2,1,0:T(8,128)S(1)}, f32[2,16,128]{2,1,0:T(8,128)S(1)}) custom-call(s32[4]{0:T(128)S(1)} %pad_add_fusion.at, f32[32,16,128]{2,1,0:T(8,128)S(1)} %collective-permute-done.8.near, f32[32,16,128]{2,1,0:T(8,128)S(1)} %collective-permute-done.9.far, ...), custom_call_target="tpu_custom_call", output_to_operand_aliasing={{0}: (3, {})} | custom-call | flops 3000000 | bytes 3000000 | tf_op jit(solution)/shard_map/k_rows2/pallas_call | solution.py:334
  56.4 0.1 collective-permute-start.10
  56.5 5.3 %collective-permute-start.11 = (f32[2,16,128]{2,1,0:T(8,128)S(1)}, f32[2,16,128]{2,1,0:T(8,128)S(1)}, u32[]{:S(2)}, u32[]{:S(2)}) collective-permute-start(f32[2,16,128]{2,1,0:T(8,128)S(1)} %get-tuple-element.55), channel_id=1, source_target_pairs={{16,32},{32,16},{48,64},{64,48},{80,96},{96,80},{17,33},{33,17},{4... | collective-permute-start | bytes 49160 | tf_op jit(solution)/shard_map/ppermute | solution.py:363
  61.7 8.2 %k_inner2.1 = (f32[8,18,2,48,128]{4,3,2,1,0:T(8,128)S(1)}, f32[8,18,2,48,128]{4,3,2,1,0:T(8,128)S(1)}, f32[8,16,32,256]{3,2,1,0:T(8,128)}) custom-call(s32[4]{0:T(128)S(1)} %pad_add_fusion.at, f32[8,18,2,48,128]{4,3,2,1,0:T(8,128)S(1)} %get-tuple-element.57.a_in, ...), custom_call_target="tpu_custom_call", output_to_operand_aliasing={{0}: (1, {}), {1}: (2, {})} | custom-call | flops 30000000 | bytes 30000000 | tf_op jit(solution)/shard_map/k_inner2/pallas_call | solution.py:334
  70.0 3.2 %k_outer2.1 = (f32[8,18,2,48,128]{4,3,2,1,0:T(8,128)S(1)}, f32[8,18,2,48,128]{4,3,2,1,0:T(8,128)S(1)}, f32[8,16,32,256]{3,2,1,0:T(8,128)}) custom-call(s32[4]{0:T(128)S(1)} %pad_add_fusion.at, f32[8,32,256]{2,1,0:T(8,128)S(1)} %collective-permute-done.6.znear, ...), custom_call_target="tpu_custom_call", output_to_operand_aliasing={{0}: (7, {}), {1}: (8, {}), {2}: (9, {})} | custom-call | flops 3000000 | bytes 3000000 | tf_op jit(solution)/shard_map/k_outer2/pallas_call | solution.py:334
  (8 shorter events, 0.0 us)
Async XLA Ops:
  5.0 9.8 %collective-permute-start.2 = (f32[42,16,128]{2,1,0:T(8,128)S(1)}, f32[42,16,128]{2,1,0:T(8,128)S(1)}, u32[]{:S(2)}, u32[]{:S(2)}) collective-permute-start(f32[42,16,128]{2,1,0:T(8,128)S(1)} %get-tuple-element.36), channel_id=1, source_target_pairs={{0,1},{1,0},{2,3},{3,2},{4,5},{5,4},{6,7},{7,6},{8,9},{9,8},{10,11... | collective-permute-start | bytes 1032200 | tf_op jit(solution)/shard_map/ppermute | solution.py:368
  5.1 14.7 %collective-permute-start.3 = (f32[42,16,128]{2,1,0:T(8,128)S(1)}, f32[42,16,128]{2,1,0:T(8,128)S(1)}, u32[]{:S(2)}, u32[]{:S(2)}) collective-permute-start(f32[42,16,128]{2,1,0:T(8,128)S(1)} %get-tuple-element.37), channel_id=1, source_target_pairs={{1,2},{2,1},{3,4},{4,3},{5,6},{6,5},{7,8},{8,7},{9,10},{10,9},{11,... | collective-permute-start | bytes 1032200 | tf_op jit(solution)/shard_map/ppermute | solution.py:367
  9.4 29.9 %collective-permute-start = (f32[8,32,256]{2,1,0:T(8,128)S(1)}, f32[8,32,256]{2,1,0:T(8,128)S(1)}, u32[]{:S(2)}, u32[]{:S(2)}) collective-permute-start(f32[8,32,256]{2,1,0:T(8,128)S(1)} %get-tuple-element.34), channel_id=1, source_target_pairs={{0,16},{16,0},{32,48},{48,32},{64,80},{80,64},{96,112},{112,96},{1... | collective-permute-start | bytes 786440 | tf_op jit(solution)/shard_map/ppermute | solution.py:364
  10.9 28.4 %collective-permute-start.1 = (f32[8,32,256]{2,1,0:T(8,128)S(1)}, f32[8,32,256]{2,1,0:T(8,128)S(1)}, u32[]{:S(2)}, u32[]{:S(2)}) collective-permute-start(f32[8,32,256]{2,1,0:T(8,128)S(1)} %get-tuple-element.35), channel_id=1, source_target_pairs={{16,32},{32,16},{48,64},{64,48},{80,96},{96,80},{17,33},{33,17},{4... | collective-permute-start | bytes 786440 | tf_op jit(solution)/shard_map/ppermute | solution.py:363
  20.9 18.5 %collective-permute-start.4 = (f32[2,56,128]{2,1,0:T(8,128)S(1)}, f32[2,56,128]{2,1,0:T(8,128)S(1)}, u32[]{:S(2)}, u32[]{:S(2)}) collective-permute-start(f32[2,56,128]{2,1,0:T(8,128)S(1)} %get-tuple-element.41), channel_id=1, source_target_pairs={{0,16},{16,0},{32,48},{48,32},{64,80},{80,64},{96,112},{112,96},{1... | collective-permute-start | bytes 172040 | tf_op jit(solution)/shard_map/ppermute | solution.py:364
  21.5 17.9 %collective-permute-start.5 = (f32[2,56,128]{2,1,0:T(8,128)S(1)}, f32[2,56,128]{2,1,0:T(8,128)S(1)}, u32[]{:S(2)}, u32[]{:S(2)}) collective-permute-start(f32[2,56,128]{2,1,0:T(8,128)S(1)} %get-tuple-element.42), channel_id=1, source_target_pairs={{16,32},{32,16},{48,64},{64,48},{80,96},{96,80},{17,33},{33,17},{4... | collective-permute-start | bytes 172040 | tf_op jit(solution)/shard_map/ppermute | solution.py:363
  42.4 9.2 %collective-permute-start.8 = (f32[32,16,128]{2,1,0:T(8,128)S(1)}, f32[32,16,128]{2,1,0:T(8,128)S(1)}, u32[]{:S(2)}, u32[]{:S(2)}) collective-permute-start(f32[32,16,128]{2,1,0:T(8,128)S(1)} %get-tuple-element.51), channel_id=1, source_target_pairs={{0,1},{1,0},{2,3},{3,2},{4,5},{5,4},{6,7},{7,6},{8,9},{9,8},{10,11... | collective-permute-start | bytes 786440 | tf_op jit(solution)/shard_map/ppermute | solution.py:368
  42.5 12.9 %collective-permute-start.9 = (f32[32,16,128]{2,1,0:T(8,128)S(1)}, f32[32,16,128]{2,1,0:T(8,128)S(1)}, u32[]{:S(2)}, u32[]{:S(2)}) collective-permute-start(f32[32,16,128]{2,1,0:T(8,128)S(1)} %get-tuple-element.52), channel_id=1, source_target_pairs={{1,2},{2,1},{3,4},{4,3},{5,6},{6,5},{7,8},{8,7},{9,10},{10,9},{11,... | collective-permute-start | bytes 786440 | tf_op jit(solution)/shard_map/ppermute | solution.py:367
  46.2 23.7 %collective-permute-start.6 = (f32[8,32,256]{2,1,0:T(8,128)S(1)}, f32[8,32,256]{2,1,0:T(8,128)S(1)}, u32[]{:S(2)}, u32[]{:S(2)}) collective-permute-start(f32[8,32,256]{2,1,0:T(8,128)S(1)} %get-tuple-element.49), channel_id=1, source_target_pairs={{0,16},{16,0},{32,48},{48,32},{64,80},{80,64},{96,112},{112,96},{1... | collective-permute-start | bytes 786440 | tf_op jit(solution)/shard_map/ppermute | solution.py:364
  46.3 23.6 %collective-permute-start.7 = (f32[8,32,256]{2,1,0:T(8,128)S(1)}, f32[8,32,256]{2,1,0:T(8,128)S(1)}, u32[]{:S(2)}, u32[]{:S(2)}) collective-permute-start(f32[8,32,256]{2,1,0:T(8,128)S(1)} %get-tuple-element.50), channel_id=1, source_target_pairs={{16,32},{32,16},{48,64},{64,48},{80,96},{96,80},{17,33},{33,17},{4... | collective-permute-start | bytes 786440 | tf_op jit(solution)/shard_map/ppermute | solution.py:363
  56.4 13.6 %collective-permute-start.10 = (f32[2,16,128]{2,1,0:T(8,128)S(1)}, f32[2,16,128]{2,1,0:T(8,128)S(1)}, u32[]{:S(2)}, u32[]{:S(2)}) collective-permute-start(f32[2,16,128]{2,1,0:T(8,128)S(1)} %get-tuple-element.54), channel_id=1, source_target_pairs={{0,16},{16,0},{32,48},{48,32},{64,80},{80,64},{96,112},{112,96},{1... | collective-permute-start | bytes 49160 | tf_op jit(solution)/shard_map/ppermute | solution.py:364
  56.5 13.5 %collective-permute-start.11 = (f32[2,16,128]{2,1,0:T(8,128)S(1)}, f32[2,16,128]{2,1,0:T(8,128)S(1)}, u32[]{:S(2)}, u32[]{:S(2)}) collective-permute-start(f32[2,16,128]{2,1,0:T(8,128)S(1)} %get-tuple-element.55), channel_id=1, source_target_pairs={{16,32},{32,16},{48,64},{64,48},{80,96},{96,80},{17,33},{33,17},{4... | collective-permute-start | bytes 49160 | tf_op jit(solution)/shard_map/ppermute | solution.py:363

commit v3 on v2

--- a/solution.py
+++ b/solution.py
@@ -117,62 +117,103 @@
         lax.fori_loop(0, L, one, 0)
 
 
-def sweep(src, dst, cf, sd, first, count, step, wide, onehot):
+MID1, EDGE1 = (15, 23, 31), (7, 33)
+MID2, EDGE2 = (16, 24), (8, 32)
+
+
+def sweep(src, dst, cf, sd, planes, starts, onehot, group=1):
     sf, df, kf, ef = flat(src), flat(dst), flat(cf), flat(sd)
-    starts = (7, 15, 23, 31, 33) if wide else (8, 16, 24, 32)
+    first, count, step = planes
+
+    def tile(p, r0):
+        at, to = p * PS, (p + 1) * PS
+        co = [[kf[pl.ds(at + (d * NP * 2 + h) * RB + r0, 8), :] for h in range(2)] for d in range(6)]
+        seed = [ef[pl.ds(at + h * RB + r0, 8), :] for h in range(2)]
+        rest = [jnp.where(s == 0, f32(1.0 - OMEGA), f32(0.0 if onehot else 1.0)) for s in seed]
+        for l in range(L):
+            base = to + l * LS + r0
+            here = [sf[pl.ds(base + h * RB, 8), :] for h in range(2)]
+            xn, xp = rolled(*here)
+            for h in range(2):
+                o = base + h * RB
+                t = co[0][h] * sf[pl.ds(o + PS, 8), :] + co[1][h] * sf[pl.ds(o - PS, 8), :]
+                t = t + (co[2][h] * sf[pl.ds(o + 1, 8), :] + co[3][h] * sf[pl.ds(o - 1, 8), :])
+                t = t + (co[4][h] * xn[h] + co[5][h] * xp[h])
+                t = t + rest[h] * here[h]
+                df[pl.ds(o, 8), :] = jnp.where(seed[h] == l + 1, 1.0, t) if onehot else t
 
     def body(i, c):
-        p = first + i * step
-        at, to = p * PS, (p + 1) * PS
-        for r0 in starts:
-            co = [[kf[pl.ds(at + (d * NP * 2 + h) * RB + r0, 8), :] for h in range(2)] for d in range(6)]
-            seed = [ef[pl.ds(at + h * RB + r0, 8), :] for h in range(2)]
-            rest = [jnp.where(s == 0, f32(1.0 - OMEGA), f32(0.0 if onehot else 1.0)) for s in seed]
-            for l in range(L):
-                base = to + l * LS + r0
-                here = [sf[pl.ds(base + h * RB, 8), :] for h in range(2)]
-                xn, xp = rolled(*here)
-                for h in range(2):
-                    o = base + h * RB
-                    t = co[0][h] * sf[pl.ds(o + PS, 8), :] + co[1][h] * sf[pl.ds(o - PS, 8), :]
-                    t = t + (co[2][h] * sf[pl.ds(o + 1, 8), :] + co[3][h] * sf[pl.ds(o - 1, 8), :])
-                    t = t + (co[4][h] * xn[h] + co[5][h] * xp[h])
-                    t = t + rest[h] * here[h]
-                    df[pl.ds(o, 8), :] = jnp.where(seed[h] == l + 1, 1.0, t) if onehot else t
+        for g in range(group):
+            for r0 in starts:
+                tile(first + (i * group + g) * step, r0)
         return c
 
-    lax.fori_loop(0, count, body, 0)
-
-
-def wide_row(i):
-    return jnp.where(i == 4, 33, 7 + 8 * i)
-
-
-def coefficients(w, sd, cf, first, count):
-    def body(i, c):
-        p, r0 = first + i // 5, wide_row(i % 5)
-        seed = [sd[p, h, pl.ds(r0, 8), :] for h in range(2)]
-        zu = [w[0, p + 1, h, pl.ds(r0, 8), :] for h in range(2)]
-        zd = [w[0, p, h, pl.ds(r0, 8), :] for h in range(2)]
-        yu = [w[1, p + 1, h, pl.ds(r0, 8), :] for h in range(2)]
-        yd = [w[1, p + 1, h, pl.ds(r0 - 1, 8), :] for h in range(2)]
-        xu = [w[2, p + 1, h, pl.ds(r0, 8), :] for h in range(2)]
-        lane = lanes()
+    lax.fori_loop(0, count // group, body, 0)
+
+
+def coefficients(w, sd, cf, first, count, starts, group=1):
+    wf, kf, ef = flat(w), flat(cf), flat(sd)
+    lane = lanes()
+
+    def tile(p, r0):
+        seed, xu = [], []
+        for h in range(2):
+            seed.append(ef[pl.ds(p * PS + h * RB + r0, 8), :])
+            xu.append(wf[pl.ds((2 * PB + p + 1) * PS + h * RB + r0, 8), :])
         pa, pb = (pltpu.roll(x, 1, 1) for x in xu)
         xd = [jnp.where(lane == 0, 0.0, pa), jnp.where(lane == 0, pa, pb)]
         for h in range(2):
-            degree = zu[h] + zd[h] + yu[h] + yd[h] + xu[h] + xd[h]
+            o = p * PS + h * RB + r0
+            zd = wf[pl.ds(o, 8), :]
+            zu = wf[pl.ds(o + PS, 8), :]
+            yu = wf[pl.ds(o + (PB + 1) * PS, 8), :]
+            yd = wf[pl.ds(o + (PB + 1) * PS - 1, 8), :]
+            degree = zu + zd + yu + yd + xu[h] + xd[h]
             live = (seed[h] == 0) & (degree > 0.0)
             scale = jnp.where(live, OMEGA / jnp.where(live, degree, 1.0), 0.0)
-            for d, x in enumerate((zu, zd, yu, yd, xu, xd)):
-                cf[d, p, h, pl.ds(r0, 8), :] = scale * x[h]
+            for d, x in enumerate((zu, zd, yu, yd, xu[h], xd[h])):
+                kf[pl.ds(o + d * NP * PS, 8), :] = scale * x
+
+    def body(i, c):
+        for g in range(group):
+            for r0 in starts:
+                tile(first + i * group + g, r0)
         return c
 
-    lax.fori_loop(0, count * 5, body, 0)
+    lax.fori_loop(0, count // group, body, 0)
+
+
+def weigh(bclass, at, lev, w, tiles, group):
+    top_slab, top_band = at[2] == 1, at[3] == 1
+    cls = bclass[0, 0]
+    beta = f32(0.0)
+    for index in range(4):
+        beta = beta + jnp.where(cls == index, f32(BETAS[index]), f32(0.0))
+    row = lax.broadcasted_iota(jnp.int32, (8, HX), 0)
+    lane = lanes()
+
+    def body(i, c):
+        for g in range(group):
+            p = i * group + g
+            for t in tiles:
+                for d in range(3):
+                    for h in range(2):
+                        ratio = lev[d, p, h, 8 * t : 8 * t + 8, :].astype(f32) / 255.0
+                        x = FLOOR + jnp.exp(-beta * ratio * ratio)
+                        if d == 0:
+                            x = jnp.where(top_slab & (p == NP - 1), 0.0, x)
+                        elif d == 1 and t == 3:
+                            x = jnp.where((row == 7) & top_band, 0.0, x)
+                        elif d == 2 and h == 1:
+                            x = jnp.where(lane == HX - 1, 0.0, x)
+                        w[d, p + 1, h, 8 * t + 8 : 8 * t + 16, :] = x
+        return c
+
+    lax.fori_loop(0, NP // group, body, 0)
 
 
 def k_load(at, bclass, prior, levels, seeds, a, w, sd, near, far, pn, pf, lev, sem):
-    even, zeven, top_slab, top_band = at[0] == 0, at[1] == 0, at[2] == 1, at[3] == 1
+    even, zeven = at[0] == 0, at[1] == 0
     copies = []
     for h in range(2):
         cols = pl.ds(h * HX, HX)
@@ -190,32 +231,9 @@
     copies.append(pltpu.make_async_copy(prior.at[:, jnp.where(zeven, 0, NP - 1)], pf, sem.at[21]))
     for c in copies:
         c.start()
-    cls = bclass[0, 0]
-    beta = f32(0.0)
-    for index in range(4):
-        beta = beta + jnp.where(cls == index, f32(BETAS[index]), f32(0.0))
     for c in copies[:4]:
         c.wait()
-    row = lax.broadcasted_iota(jnp.int32, (8, HX), 0)
-    lane = lanes()
-
-    def weigh(i, c):
-        p, t = i // 4, i % 4
-        r0 = pl.multiple_of(8 * t, 8)
-        for d in range(3):
-            for h in range(2):
-                ratio = lev[d, p, h, pl.ds(r0, 8), :].astype(f32) / 255.0
-                x = FLOOR + jnp.exp(-beta * ratio * ratio)
-                if d == 0:
-                    x = jnp.where(top_slab & (p == NP - 1), 0.0, x)
-                elif d == 1:
-                    x = jnp.where((row == 7) & (top_band & (t == 3)), 0.0, x)
-                elif h == 1:
-                    x = jnp.where(lane == HX - 1, 0.0, x)
-                w[d, p + 1, h, pl.ds(r0 + 8, 8), :] = x
-        return c
-
-    lax.fori_loop(0, NP * 4, weigh, 0)
+    weigh(bclass, at, lev, w, (0, 3), 2)
     for c in copies[4:]:
         c.wait()
     pack_rows(a, even, near, far, 21)
@@ -254,10 +272,17 @@
                 out[h, r0 + 9 : r0 + 17, :] = w[0, NP, h, r0 : r0 + 8, :]
 
 
-def k_inner(at, a_in, w, sd, a, b, cf):
-    coefficients(w, sd, cf, 1, NP - 1)
-    sweep(a, b, cf, sd, 1, NP - 2, 1, True, True)
-    sweep(b, a, cf, sd, 2, NP - 4, 1, False, False)
+def k_mid(at, bclass, lev, a_in, w_in, sd, a, w, b, cf):
+    weigh(bclass, at, lev, w, (1, 2), 2)
+    coefficients(w, sd, cf, 1, NP - 1, MID1, 1)
+    sweep(a, b, cf, sd, (1, NP - 2, 1), MID1, True, 2)
+    sweep(b, a, cf, sd, (2, NP - 4, 1), MID2, False, 3)
+
+
+def k_edge(at, a_in, b_in, cf_in, w, sd, a, b, cf):
+    coefficients(w, sd, cf, 1, NP - 1, EDGE1, 3)
+    sweep(a, b, cf, sd, (1, NP - 2, 1), EDGE1, True, 2)
+    sweep(b, a, cf, sd, (2, NP - 4, 1), EDGE2, False, 3)
 
 
 def k_outer(at, znear, zfar, cnear, cfar, w_in, sd, a_in, b_in, cf_in, w, a, b, cf, near, far, pnear, pfar):
@@ -269,10 +294,10 @@
             r0 = 7 + 8 * t if t < 4 else 33
             cut = slice(r0 + 9, r0 + 17)
             w[0, 0, h, r0 : r0 + 8, :] = jnp.where(zeven, cfar[h, cut, :], cnear[h, cut, :])
-    coefficients(w, sd, cf, 0, 1)
-    sweep(a, b, cf, sd, 0, 2, NP - 1, True, True)
-    sweep(b, a, cf, sd, 0, 2, 1, False, False)
-    sweep(b, a, cf, sd, NP - 2, 2, 1, False, False)
+    coefficients(w, sd, cf, 0, 1, MID1 + EDGE1)
+    sweep(a, b, cf, sd, (0, 2, NP - 1), MID1 + EDGE1, True)
+    sweep(b, a, cf, sd, (0, 2, 1), MID2 + EDGE2, False)
+    sweep(b, a, cf, sd, (NP - 2, 2, 1), MID2 + EDGE2, False)
     pack_planes(a, zeven, pnear, pfar)
     pack_rows(a, even, near, far, 16)
 
@@ -301,9 +326,14 @@
         c.wait()
 
 
-def k_inner2(at, a_in, b_in, cf, sd, a, b, out, sem):
-    sweep(a, b, cf, sd, 1, NP - 2, 1, True, False)
-    sweep(b, a, cf, sd, 2, NP - 4, 1, False, False)
+def k_mid2(at, a_in, b_in, cf, sd, a, b):
+    sweep(a, b, cf, sd, (1, NP - 2, 1), MID1, False, 2)
+    sweep(b, a, cf, sd, (2, NP - 4, 1), MID2, False, 3)
+
+
+def k_edge2(at, a_in, b_in, cf, sd, a, b, out, sem):
+    sweep(a, b, cf, sd, (1, NP - 2, 1), EDGE1, False, 2)
+    sweep(b, a, cf, sd, (2, NP - 4, 1), EDGE2, False, 3)
     put(a, out, sem, ((2, NP - 4),))
 
 
@@ -311,9 +341,9 @@
     zeven = at[1] == 0
     unpack_planes(a, b, zeven, znear, zfar)
     unpack_corners(a, zeven, cnear, cfar)
-    sweep(a, b, cf, sd, 0, 2, NP - 1, True, False)
-    sweep(b, a, cf, sd, 0, 2, 1, False, False)
-    sweep(b, a, cf, sd, NP - 2, 2, 1, False, False)
+    sweep(a, b, cf, sd, (0, 2, NP - 1), MID1 + EDGE1, False)
+    sweep(b, a, cf, sd, (0, 2, 1), MID2 + EDGE2, False)
+    sweep(b, a, cf, sd, (NP - 2, 2, 1), MID2 + EDGE2, False)
     put(a, out, sem, ((0, 2), (NP - 2, 2)))
 
 
@@ -371,15 +401,22 @@
     sds = jax.ShapeDtypeStruct
     rows = sds((42, NP, HX), f32)
     plane = sds((L, NR, 2 * HX), f32)
-    a, w, sd, near, far, pn, pf = call(
+    a, w, sd, near, far, pn, pf, lev = call(
         k_load,
         [("s", at), ("s", bclass), ("a", prior), ("a", levels), ("a", seeds)],
-        [("v", vmem(A_SHAPE)), ("v", vmem(W_SHAPE)), ("v", vmem(S_SHAPE, jnp.int32)), ("v", rows), ("v", rows), ("v", plane), ("v", plane)],
-        scratch=[pltpu.VMEM((3, NP, 2, NR, HX), jnp.int32), pltpu.SemaphoreType.DMA((22,))],
-        grant=8,
+        [("v", vmem(A_SHAPE)), ("v", vmem(W_SHAPE)), ("v", vmem(S_SHAPE, jnp.int32)), ("v", rows), ("v", rows), ("v", plane), ("v", plane)]
+        + [("v", vmem((3, NP, 2, NR, HX), jnp.int32))],
+        scratch=[pltpu.SemaphoreType.DMA((22,))],
     )
     near, far = yswap(near, far)
     zn, zf = zswap(pn, pf)
+    a, w, b, cf = call(
+        k_mid,
+        [("s", at), ("s", bclass), ("v", lev), ("v", a), ("v", w), ("v", sd)],
+        [("v", vmem(A_SHAPE)), ("v", vmem(W_SHAPE)), ("v", vmem(A_SHAPE)), ("v", vmem(C_SHAPE))],
+        aliases={3: 0, 4: 1},
+        cost=30000000,
+    )
     corner = sds((2, 56, HX), f32)
     a, w, sd, cn, cf_ = call(
         k_rows,
@@ -389,10 +426,10 @@
     )
     cn, cf_ = zswap(cn, cf_)
     a, b, cf = call(
-        k_inner,
-        [("s", at), ("v", a), ("v", w), ("v", sd)],
+        k_edge,
+        [("s", at), ("v", a), ("v", b), ("v", cf), ("v", w), ("v", sd)],
         [("v", vmem(A_SHAPE)), ("v", vmem(A_SHAPE)), ("v", vmem(C_SHAPE))],
-        aliases={1: 0},
+        aliases={1: 0, 2: 1, 3: 2},
         cost=30000000,
     )
     rows = sds((32, NP, HX), f32)
@@ -405,6 +442,13 @@
     )
     near, far = yswap(near, far)
     zn, zf = zswap(pn, pf)
+    a, b = call(
+        k_mid2,
+        [("s", at), ("v", a), ("v", b), ("v", cf), ("v", sd)],
+        [("v", vmem(A_SHAPE)), ("v", vmem(A_SHAPE))],
+        aliases={1: 0, 2: 1},
+        cost=30000000,
+    )
     corner = sds((2, 16, HX), f32)
     a, cn, cf_ = call(
         k_rows2,
@@ -415,7 +459,7 @@
     cn, cf_ = zswap(cn, cf_)
     whole = sds(prior.shape, f32)
     a, b, out = call(
-        k_inner2,
+        k_edge2,
         [("s", at), ("v", a), ("v", b), ("v", cf), ("v", sd)],
         [("v", vmem(A_SHAPE)), ("v", vmem(A_SHAPE)), ("a", whole)],
         aliases={1: 0, 2: 1},

time: 73.5 us -> 64.3 us (0.87)
  Pallas kernels: 33.9 us -> 29.6 us
  waiting for transfers between devices: 8.78 us -> 4.95 us
  starting transfers between devices: 29.6 us -> 28.6 us
    ppermute x2, waiting for transfers between devices: 8.75 us -> 1.25 us  [yswap(): far = lax.ppermute(far, 'gy', yfar_)]
    pallas_call x7 -> x9, Pallas kernels: 33.9 us -> 29.6 us  [call(): pl.pallas_call(kernel, out_shape=tuple((o for _, o in outs)), in_specs=sp...]
    ppermute x4, waiting for transfers between devices: 0.01 us -> 3.69 us  [zswap(): far = lax.ppermute(far, 'gz', zfar_)]
    ppermute x2, starting transfers between devices: 8.04 us -> 6.98 us  [yswap(): far = lax.ppermute(far, 'gy', yfar_)]
  transfers between devices with their start and end apart: 12 -> 12, of which waited for: 2 -> 3; matrix products, arithmetic and copies ran while one was open for 0% -> 0% of each run, Pallas kernels for 32% -> 30%
where the time goes in v3:
time: 64.3 us; the launch traced here: 64.1 us
  Pallas kernels  29.6 us (46%)
  starting transfers between devices  28.6 us (44%)
  waiting for transfers between devices  4.95 us (8%)
  between operations  0.85 us (1%)
    pallas_call x9, Pallas kernels, call(): pl.pallas_call(kernel, out_shape=tuple((o for _, o in outs)), in_specs=sp...  29.6 us
    ppermute x4, starting transfers between devices, zswap(): far = lax.ppermute(far, 'gz', zfar_)  19.3 us
    ppermute x2, starting transfers between devices, yswap(): far = lax.ppermute(far, 'gy', yfar_)  6.98 us
    ppermute x4, waiting for transfers between devices, zswap(): far = lax.ppermute(far, 'gz', zfar_)  3.69 us
    ppermute x4, starting transfers between devices, zswap(): return (lax.ppermute(near, 'gz', znear_), far)  2.09 us
  transfers between devices with their start and end apart: 12, of which 3 were waited for; matrix products, arithmetic and copies ran while one was open for 0% of the time, Pallas kernels for 30%

profile of v3, /device:TPU:26, one launch (start us, length us, event | category | flops | bytes accessed | tf_op | source)
XLA Modules:
  0.0 64.1 jit_solution(5866082387263428369)
XLA Ops:
  0.7 4.3 %k_load.1 = (f32[8,18,2,48,128]{4,3,2,1,0:T(8,128)S(1)}, f32[3,18,2,48,128]{4,3,2,1,0:T(8,128)S(1)}, s32[16,2,48,128]{3,2,1,0:T(8,128)S(1)}, f32[42,16,128]{2,1,...) custom-call(s32[4]{0:T(128)S(1)} %pad_add_fusion.at, ...), custom_call_target="tpu_custom_call" | custom-call | flops 3000000 | bytes 3000000 | tf_op jit(solution)/shard_map/k_load/pallas_call | solution.py:364
  5.0 0.1 collective-permute-start.2
  5.1 4.3 %collective-permute-start.3 = (f32[42,16,128]{2,1,0:T(8,128)S(1)}, f32[42,16,128]{2,1,0:T(8,128)S(1)}, u32[]{:S(2)}, u32[]{:S(2)}) collective-permute-start(f32[42,16,128]{2,1,0:T(8,128)S(1)} %get-tuple-element.44), channel_id=1, source_target_pairs={{1,2},{2,1},{3,4},{4,3},{5,6},{6,5},{7,8},{8,7},{9,10},{10,9},{11,... | collective-permute-start | bytes 1032200 | tf_op jit(solution)/shard_map/ppermute | solution.py:397
  9.4 1.5 %collective-permute-start = (f32[8,32,256]{2,1,0:T(8,128)S(1)}, f32[8,32,256]{2,1,0:T(8,128)S(1)}, u32[]{:S(2)}, u32[]{:S(2)}) collective-permute-start(f32[8,32,256]{2,1,0:T(8,128)S(1)} %get-tuple-element.41), channel_id=1, source_target_pairs={{0,16},{16,0},{32,48},{48,32},{64,80},{80,64},{96,112},{112,96},{1... | collective-permute-start | bytes 786440 | tf_op jit(solution)/shard_map/ppermute | solution.py:394
  10.9 3.8 %collective-permute-start.1 = (f32[8,32,256]{2,1,0:T(8,128)S(1)}, f32[8,32,256]{2,1,0:T(8,128)S(1)}, u32[]{:S(2)}, u32[]{:S(2)}) collective-permute-start(f32[8,32,256]{2,1,0:T(8,128)S(1)} %get-tuple-element.42), channel_id=1, source_target_pairs={{16,32},{32,16},{48,64},{64,48},{80,96},{96,80},{17,33},{33,17},{4... | collective-permute-start | bytes 786440 | tf_op jit(solution)/shard_map/ppermute | solution.py:393
  14.8 5.3 %k_mid.1 = (f32[8,18,2,48,128]{4,3,2,1,0:T(8,128)S(1)}, f32[3,18,2,48,128]{4,3,2,1,0:T(8,128)S(1)}, f32[8,18,2,48,128]{4,3,2,1,0:T(8,128)S(1)}, f32[6,16,2,48,128]{4,3,2,1,0:T(8,128)S(1)}) custom-call(s32[4]{0:T(128)S(1)} %pad_add_fusion.at, s32[1,1]{1,0:T(1,128)S(6)} %copy.45.bclass, ...), custom_call_target="tpu_custom_call", output_to_operand_aliasing={{0}: (3, {}), {1}: (4, {})} | custom-call | flops 30000000 | bytes 30000000 | tf_op jit(solution)/shard_map/k_mid/pallas_call | solution.py:364
  20.1 1.1 %k_rows.1 = (f32[8,18,2,48,128]{4,3,2,1,0:T(8,128)S(1)}, f32[3,18,2,48,128]{4,3,2,1,0:T(8,128)S(1)}, s32[16,2,48,128]{3,2,1,0:T(8,128)S(1)}, f32[2,56,128]{2,1,0:T(8,128)S(1)}, f32[2,56,128]{2,1,0:T(8,128)S(1)}) custom-call(s32[4]{0:T(128)S(1)} %pad_add_fusion.at, ...), custom_call_target="tpu_custom_call", output_to_operand_aliasing={{0}: (3, {}), {1}: (4, {}), {2}: (5, {})} | custom-call | flops 3000000 | bytes 3000000 | tf_op jit(solution)/shard_map/k_rows/pallas_call | solution.py:364
  21.2 0.3 collective-permute-start.4
  21.5 5.1 %collective-permute-start.5 = (f32[2,56,128]{2,1,0:T(8,128)S(1)}, f32[2,56,128]{2,1,0:T(8,128)S(1)}, u32[]{:S(2)}, u32[]{:S(2)}) collective-permute-start(f32[2,56,128]{2,1,0:T(8,128)S(1)} %get-tuple-element.52), channel_id=1, source_target_pairs={{16,32},{32,16},{48,64},{64,48},{80,96},{96,80},{17,33},{33,17},{4... | collective-permute-start | bytes 172040 | tf_op jit(solution)/shard_map/ppermute | solution.py:393
  26.6 3.7 %k_edge.1 = (f32[8,18,2,48,128]{4,3,2,1,0:T(8,128)S(1)}, f32[8,18,2,48,128]{4,3,2,1,0:T(8,128)S(1)}, f32[6,16,2,48,128]{4,3,2,1,0:T(8,128)S(1)}) custom-call(s32[4]{0:T(128)S(1)} %pad_add_fusion.at, f32[8,18,2,48,128]{4,3,2,1,0:T(8,128)S(1)} %get-tuple-element.55.a_in, ...), custom_call_target="tpu_custom_call", output_to_operand_aliasing={{0}: (1, {}), {1}: (2, {}), {2}: (3, {})} | custom-call | flops 30000000 | bytes 30000000 | tf_op jit(solution)/shard_map/k_edge/pallas_call | solution.py:364
  30.3 2.1 %collective-permute-done.1.zfar = f32[8,32,256]{2,1,0:T(8,128)S(1)} collective-permute-done((f32[8,32,256]{2,1,0:T(8,128)S(1)}, f32[8,32,256]{2,1,0:T(8,128)S(1)}, u32[]{:S(2)}, u32[]{:S(2)}) %collective-permute-start.1) | collective-permute-done | bytes 262176 | tf_op jit(solution)/shard_map/ppermute | solution.py:393
  32.3 1.6 %collective-permute-done.5.cfar = f32[2,56,128]{2,1,0:T(8,128)S(1)} collective-permute-done((f32[2,56,128]{2,1,0:T(8,128)S(1)}, f32[2,56,128]{2,1,0:T(8,128)S(1)}, u32[]{:S(2)}, u32[]{:S(2)}) %collective-permute-start.5) | collective-permute-done | bytes 57376 | tf_op jit(solution)/shard_map/ppermute | solution.py:393
  33.9 2.6 %k_outer.1 = (f32[3,18,2,48,128]{4,3,2,1,0:T(8,128)S(1)}, f32[8,18,2,48,128]{4,3,2,1,0:T(8,128)S(1)}, f32[8,18,2,48,128]{4,3,2,1,0:T(8,128)S(1)}, f32[6,16,2,48,...) custom-call(s32[4]{0:T(128)S(1)} %pad_add_fusion.at, ...), custom_call_target="tpu_custom_call", output_to_operand_aliasing={{0}: (5, {}), {1}: (7, {}), {2}: (8, {}), {3}: (9, {})} | custom-call | flops 3000000 | bytes 3000000 | tf_op jit(solution)/shard_map/k_outer/pallas_call | solution.py:364
  36.6 0.1 collective-permute-start.8
  36.7 2.7 %collective-permute-start.9 = (f32[32,16,128]{2,1,0:T(8,128)S(1)}, f32[32,16,128]{2,1,0:T(8,128)S(1)}, u32[]{:S(2)}, u32[]{:S(2)}) collective-permute-start(f32[32,16,128]{2,1,0:T(8,128)S(1)} %get-tuple-element.64), channel_id=1, source_target_pairs={{1,2},{2,1},{3,4},{4,3},{5,6},{6,5},{7,8},{8,7},{9,10},{10,9},{11,... | collective-permute-start | bytes 786440 | tf_op jit(solution)/shard_map/ppermute | solution.py:397
  39.3 0.2 collective-permute-start.6
  39.5 5.2 %collective-permute-start.7 = (f32[8,32,256]{2,1,0:T(8,128)S(1)}, f32[8,32,256]{2,1,0:T(8,128)S(1)}, u32[]{:S(2)}, u32[]{:S(2)}) collective-permute-start(f32[8,32,256]{2,1,0:T(8,128)S(1)} %get-tuple-element.62), channel_id=1, source_target_pairs={{16,32},{32,16},{48,64},{64,48},{80,96},{96,80},{17,33},{33,17},{4... | collective-permute-start | bytes 786440 | tf_op jit(solution)/shard_map/ppermute | solution.py:393
  44.7 3.6 %k_mid2.1 = (f32[8,18,2,48,128]{4,3,2,1,0:T(8,128)S(1)}, f32[8,18,2,48,128]{4,3,2,1,0:T(8,128)S(1)}) custom-call(s32[4]{0:T(128)S(1)} %pad_add_fusion.at, f32[8,18,2,48,128]{4,3,2,1,0:T(8,128)S(1)} %get-tuple-element.65.a_in, f32[8,18,2,48,128]{4,3,2,1,0:T(8,128)S(1)} %get-tuple-element.66.b_in, ...), custom_call_target="tpu_custom_call", output_to_operand_aliasing={{0}: (1, {}), {1}: (2, {})} | custom-call | flops 30000000 | bytes 30000000 | tf_op jit(solution)/shard_map/k_mid2/pallas_call | solution.py:364
  48.3 1.2 %collective-permute-done.9.far = f32[32,16,128]{2,1,0:T(8,128)S(1)} collective-permute-done((f32[32,16,128]{2,1,0:T(8,128)S(1)}, f32[32,16,128]{2,1,0:T(8,128)S(1)}, u32[]{:S(2)}, u32[]{:S(2)}) %collective-permute-start.9) | collective-permute-done | bytes 262176 | tf_op jit(solution)/shard_map/ppermute | solution.py:397
  49.6 1.0 %k_rows2.1 = (f32[8,18,2,48,128]{4,3,2,1,0:T(8,128)S(1)}, f32[2,16,128]{2,1,0:T(8,128)S(1)}, f32[2,16,128]{2,1,0:T(8,128)S(1)}) custom-call(s32[4]{0:T(128)S(1)} %pad_add_fusion.at, f32[32,16,128]{2,1,0:T(8,128)S(1)} %collective-permute-done.8.near, f32[32,16,128]{2,1,0:T(8,128)S(1)} %collective-permute-done.9.far, ...), custom_call_target="tpu_custom_call", output_to_operand_aliasing={{0}: (3, {})} | custom-call | flops 3000000 | bytes 3000000 | tf_op jit(solution)/shard_map/k_rows2/pallas_call | solution.py:364
  50.6 0.1 collective-permute-start.10
  50.7 5.3 %collective-permute-start.11 = (f32[2,16,128]{2,1,0:T(8,128)S(1)}, f32[2,16,128]{2,1,0:T(8,128)S(1)}, u32[]{:S(2)}, u32[]{:S(2)}) collective-permute-start(f32[2,16,128]{2,1,0:T(8,128)S(1)} %get-tuple-element.70), channel_id=1, source_target_pairs={{16,32},{32,16},{48,64},{64,48},{80,96},{96,80},{17,33},{33,17},{4... | collective-permute-start | bytes 49160 | tf_op jit(solution)/shard_map/ppermute | solution.py:393
  55.9 4.9 %k_edge2.1 = (f32[8,18,2,48,128]{4,3,2,1,0:T(8,128)S(1)}, f32[8,18,2,48,128]{4,3,2,1,0:T(8,128)S(1)}, f32[8,16,32,256]{3,2,1,0:T(8,128)}) custom-call(s32[4]{0:T(128)S(1)} %pad_add_fusion.at, f32[8,18,2,48,128]{4,3,2,1,0:T(8,128)S(1)} %get-tuple-element.71.a_in, ...), custom_call_target="tpu_custom_call", output_to_operand_aliasing={{0}: (1, {}), {1}: (2, {})} | custom-call | flops 30000000 | bytes 30000000 | tf_op jit(solution)/shard_map/k_edge2/pallas_call | solution.py:364
  60.9 3.2 %k_outer2.1 = (f32[8,18,2,48,128]{4,3,2,1,0:T(8,128)S(1)}, f32[8,18,2,48,128]{4,3,2,1,0:T(8,128)S(1)}, f32[8,16,32,256]{3,2,1,0:T(8,128)}) custom-call(s32[4]{0:T(128)S(1)} %pad_add_fusion.at, f32[8,32,256]{2,1,0:T(8,128)S(1)} %collective-permute-done.6.znear, ...), custom_call_target="tpu_custom_call", output_to_operand_aliasing={{0}: (7, {}), {1}: (8, {}), {2}: (9, {})} | custom-call | flops 3000000 | bytes 3000000 | tf_op jit(solution)/shard_map/k_outer2/pallas_call | solution.py:364
  (10 shorter events, 0.1 us)
Async XLA Ops:
  5.0 15.1 %collective-permute-start.2 = (f32[42,16,128]{2,1,0:T(8,128)S(1)}, f32[42,16,128]{2,1,0:T(8,128)S(1)}, u32[]{:S(2)}, u32[]{:S(2)}) collective-permute-start(f32[42,16,128]{2,1,0:T(8,128)S(1)} %get-tuple-element.43), channel_id=1, source_target_pairs={{0,1},{1,0},{2,3},{3,2},{4,5},{5,4},{6,7},{7,6},{8,9},{9,8},{10,11... | collective-permute-start | bytes 1032200 | tf_op jit(solution)/shard_map/ppermute | solution.py:398
  5.1 15.0 %collective-permute-start.3 = (f32[42,16,128]{2,1,0:T(8,128)S(1)}, f32[42,16,128]{2,1,0:T(8,128)S(1)}, u32[]{:S(2)}, u32[]{:S(2)}) collective-permute-start(f32[42,16,128]{2,1,0:T(8,128)S(1)} %get-tuple-element.44), channel_id=1, source_target_pairs={{1,2},{2,1},{3,4},{4,3},{5,6},{6,5},{7,8},{8,7},{9,10},{10,9},{11,... | collective-permute-start | bytes 1032200 | tf_op jit(solution)/shard_map/ppermute | solution.py:397
  9.4 20.8 %collective-permute-start = (f32[8,32,256]{2,1,0:T(8,128)S(1)}, f32[8,32,256]{2,1,0:T(8,128)S(1)}, u32[]{:S(2)}, u32[]{:S(2)}) collective-permute-start(f32[8,32,256]{2,1,0:T(8,128)S(1)} %get-tuple-element.41), channel_id=1, source_target_pairs={{0,16},{16,0},{32,48},{48,32},{64,80},{80,64},{96,112},{112,96},{1... | collective-permute-start | bytes 786440 | tf_op jit(solution)/shard_map/ppermute | solution.py:394
  10.9 21.4 %collective-permute-start.1 = (f32[8,32,256]{2,1,0:T(8,128)S(1)}, f32[8,32,256]{2,1,0:T(8,128)S(1)}, u32[]{:S(2)}, u32[]{:S(2)}) collective-permute-start(f32[8,32,256]{2,1,0:T(8,128)S(1)} %get-tuple-element.42), channel_id=1, source_target_pairs={{16,32},{32,16},{48,64},{64,48},{80,96},{96,80},{17,33},{33,17},{4... | collective-permute-start | bytes 786440 | tf_op jit(solution)/shard_map/ppermute | solution.py:393
  21.2 11.1 %collective-permute-start.4 = (f32[2,56,128]{2,1,0:T(8,128)S(1)}, f32[2,56,128]{2,1,0:T(8,128)S(1)}, u32[]{:S(2)}, u32[]{:S(2)}) collective-permute-start(f32[2,56,128]{2,1,0:T(8,128)S(1)} %get-tuple-element.51), channel_id=1, source_target_pairs={{0,16},{16,0},{32,48},{48,32},{64,80},{80,64},{96,112},{112,96},{1... | collective-permute-start | bytes 172040 | tf_op jit(solution)/shard_map/ppermute | solution.py:394
  21.5 12.4 %collective-permute-start.5 = (f32[2,56,128]{2,1,0:T(8,128)S(1)}, f32[2,56,128]{2,1,0:T(8,128)S(1)}, u32[]{:S(2)}, u32[]{:S(2)}) collective-permute-start(f32[2,56,128]{2,1,0:T(8,128)S(1)} %get-tuple-element.52), channel_id=1, source_target_pairs={{16,32},{32,16},{48,64},{64,48},{80,96},{96,80},{17,33},{33,17},{4... | collective-permute-start | bytes 172040 | tf_op jit(solution)/shard_map/ppermute | solution.py:393
  36.6 11.7 %collective-permute-start.8 = (f32[32,16,128]{2,1,0:T(8,128)S(1)}, f32[32,16,128]{2,1,0:T(8,128)S(1)}, u32[]{:S(2)}, u32[]{:S(2)}) collective-permute-start(f32[32,16,128]{2,1,0:T(8,128)S(1)} %get-tuple-element.63), channel_id=1, source_target_pairs={{0,1},{1,0},{2,3},{3,2},{4,5},{5,4},{6,7},{7,6},{8,9},{9,8},{10,11... | collective-permute-start | bytes 786440 | tf_op jit(solution)/shard_map/ppermute | solution.py:398
  36.7 12.9 %collective-permute-start.9 = (f32[32,16,128]{2,1,0:T(8,128)S(1)}, f32[32,16,128]{2,1,0:T(8,128)S(1)}, u32[]{:S(2)}, u32[]{:S(2)}) collective-permute-start(f32[32,16,128]{2,1,0:T(8,128)S(1)} %get-tuple-element.64), channel_id=1, source_target_pairs={{1,2},{2,1},{3,4},{4,3},{5,6},{6,5},{7,8},{8,7},{9,10},{10,9},{11,... | collective-permute-start | bytes 786440 | tf_op jit(solution)/shard_map/ppermute | solution.py:397
  39.3 21.5 %collective-permute-start.6 = (f32[8,32,256]{2,1,0:T(8,128)S(1)}, f32[8,32,256]{2,1,0:T(8,128)S(1)}, u32[]{:S(2)}, u32[]{:S(2)}) collective-permute-start(f32[8,32,256]{2,1,0:T(8,128)S(1)} %get-tuple-element.61), channel_id=1, source_target_pairs={{0,16},{16,0},{32,48},{48,32},{64,80},{80,64},{96,112},{112,96},{1... | collective-permute-start | bytes 786440 | tf_op jit(solution)/shard_map/ppermute | solution.py:394
  39.5 21.3 %collective-permute-start.7 = (f32[8,32,256]{2,1,0:T(8,128)S(1)}, f32[8,32,256]{2,1,0:T(8,128)S(1)}, u32[]{:S(2)}, u32[]{:S(2)}) collective-permute-start(f32[8,32,256]{2,1,0:T(8,128)S(1)} %get-tuple-element.62), channel_id=1, source_target_pairs={{16,32},{32,16},{48,64},{64,48},{80,96},{96,80},{17,33},{33,17},{4... | collective-permute-start | bytes 786440 | tf_op jit(solution)/shard_map/ppermute | solution.py:393
  50.6 10.3 %collective-permute-start.10 = (f32[2,16,128]{2,1,0:T(8,128)S(1)}, f32[2,16,128]{2,1,0:T(8,128)S(1)}, u32[]{:S(2)}, u32[]{:S(2)}) collective-permute-start(f32[2,16,128]{2,1,0:T(8,128)S(1)} %get-tuple-element.69), channel_id=1, source_target_pairs={{0,16},{16,0},{32,48},{48,32},{64,80},{80,64},{96,112},{112,96},{1... | collective-permute-start | bytes 49160 | tf_op jit(solution)/shard_map/ppermute | solution.py:394
  50.7 10.2 %collective-permute-start.11 = (f32[2,16,128]{2,1,0:T(8,128)S(1)}, f32[2,16,128]{2,1,0:T(8,128)S(1)}, u32[]{:S(2)}, u32[]{:S(2)}) collective-permute-start(f32[2,16,128]{2,1,0:T(8,128)S(1)} %get-tuple-element.70), channel_id=1, source_target_pairs={{16,32},{32,16},{48,64},{64,48},{80,96},{96,80},{17,33},{33,17},{4... | collective-permute-start | bytes 49160 | tf_op jit(solution)/shard_map/ppermute | solution.py:393
